TPU v7x, 128 devices: a whole 4x4x4 slice. The times are simulated.
128 devices in a mesh: row: 8 (over x_lo, y), col: 8 (over z, core), feat: 2 (over x_hi).
Axes of the slice: x: 4 (x_hi: 2, x_lo: 2; x = x_hi * 2 + x_lo), y: 4, z: 4, core: 2. Of those that a mesh axis runs over, the one named last changes fastest.
Arguments:
- points: bfloat16 [4, 8, 512, 1024], P(None, 'row', None, ('col', 'feat')), may hold values from -2 to 2
- point_noise: float32 [4, 8, 512], P(None, 'row'), may hold values from 0.1 to 1
Outputs:
- schur_tiles: float32 [4, 8, 512, 4, 8, 512], P(None, 'row', None, None, 'col', 'feat')
- trace_mean: float32 [], replicated
- log_diagonal: float32 [], replicated
All inputs are finite; a program needn't handle non-finite values.
Results may differ from a plain program's by a relative error of at most 0.003.
Values may be sent and summed in bfloat16 or wider, within the bound.
A program may use at most 128 MiB of HBM per device.

v0:
```python
import functools

import jax
import jax.numpy as jnp
from jax import lax
from jax.sharding import Mesh
from jax.sharding import PartitionSpec as P

ROW = ("row_0", "row_1")
COL = ("col_0", "col_1")
COL_FEAT = ("col_0", "col_1", "feat")
ROW_COL_FEAT = ("row_0", "row_1", "col_0", "col_1", "feat")


def broadcast(value, axis, root):
    return lax.dynamic_index_in_dim(lax.all_gather(value, axis), root, 0, keepdims=False)


def over_axes(value, axes):
    return functools.reduce(lax.psum, axes, value)


def shards(points, point_noise):
    row_count = lax.axis_size(ROW)
    feat_count = lax.axis_size("feat")
    row_index = lax.axis_index(ROW)
    col_index = lax.axis_index(COL)
    feat_index = lax.axis_index("feat")
    row_points = lax.all_gather(points, COL_FEAT, axis=3, tiled=True)[:, 0]
    local_tiles, tile_size, features = row_points.shape
    col_width = tile_size // feat_count
    col_start = feat_index * col_width
    own_noise = point_noise[:, 0]
    leading, leading_noise = (
        broadcast(row_points[0], ROW, 0),
        broadcast(own_noise[0].astype(jnp.bfloat16), ROW, 0).astype(jnp.float32),
    )
    half_rows = lax.dynamic_slice_in_dim(row_points, col_start, col_width, 1)
    gathered = lax.all_gather(half_rows[None], ROW, axis=0, tiled=True)
    col_points = lax.dynamic_index_in_dim(gathered, col_index, 0, keepdims=False)
    noise_matrix = jnp.diag(leading_noise)
    leading_gram = jnp.dot(leading, leading.T, preferred_element_type=jnp.float32) + noise_matrix
    factor = jnp.linalg.cholesky(leading_gram)
    inverse = jax.scipy.linalg.solve_triangular(
        factor, jnp.eye(tile_size, dtype=jnp.float32), lower=True
    )
    row_first = jnp.dot(
        row_points.reshape(-1, features), leading.T, preferred_element_type=jnp.float32
    )
    row_first = row_first.at[:tile_size].add(jnp.where(row_index == 0, noise_matrix, 0.0))
    row_panel = jnp.dot(row_first, inverse.T, precision=lax.Precision.HIGHEST).reshape(
        local_tiles, tile_size, tile_size
    )
    col_first = jnp.dot(
        col_points.reshape(-1, features), leading.T, preferred_element_type=jnp.float32
    )
    noise_band = lax.dynamic_slice_in_dim(noise_matrix, col_start, col_width, 0)
    col_first = col_first.at[:col_width].add(jnp.where(col_index == 0, noise_band, 0.0))
    col_panel = jnp.dot(col_first, inverse.T, precision=lax.Precision.HIGHEST).reshape(
        local_tiles, col_width, tile_size
    )
    row_tile = jnp.arange(local_tiles, dtype=jnp.int32) * row_count + row_index
    col_tile = jnp.arange(local_tiles, dtype=jnp.int32) * row_count + col_index
    lower_mask = row_tile[:, None] >= col_tile[None, :]
    gram_tiles = jnp.einsum(
        "lif,mjf->limj", row_points, col_points, preferred_element_type=jnp.float32
    )
    update = jnp.einsum("lit,mjt->limj", row_panel, col_panel, precision=lax.Precision.HIGHEST)
    schur_part = gram_tiles - update
    selector = (
        jnp.arange(tile_size)[:, None] == col_start + jnp.arange(col_width)[None, :]
    ).astype(jnp.float32)
    noise_cols = lax.dynamic_slice_in_dim(own_noise, col_start, col_width, 1)
    same_tile = (row_tile[:, None] == col_tile[None, :]).astype(jnp.float32)
    schur_part = (
        schur_part
        + same_tile[:, None, :, None] * selector[None, :, None, :] * noise_cols[:, None, None, :]
    )
    panel_slice = lax.dynamic_slice_in_dim(row_panel, col_start, col_width, 2)
    first_column = col_tile == 0
    schur_part = jnp.where(
        first_column[None, None, :, None], panel_slice[:, :, None, :], schur_part
    )
    schur_part = jnp.where(lower_mask[:, None, :, None], schur_part, 0.0)
    trace_weight = same_tile * (row_tile >= 1).astype(jnp.float32)[:, None]
    partial_trace = jnp.sum(
        schur_part * trace_weight[:, None, :, None] * selector[None, :, None, :]
    )
    total_trace = over_axes(partial_trace, ROW_COL_FEAT)
    point_count = local_tiles * row_count * tile_size
    trace_mean = total_trace / jnp.float32(point_count - tile_size)
    log_diagonal = 2.0 * jnp.sum(jnp.log(jnp.diagonal(factor)))
    schur_tiles = schur_part.reshape(local_tiles, 1, tile_size, local_tiles, 1, col_width)
    return (schur_tiles, trace_mean, log_diagonal)


def solution(mesh):
    torus = Mesh(
        mesh.devices.reshape(2, 4, 4, 2, mesh.shape["feat"]),
        ("row_0", "row_1", "col_0", "col_1", "feat"),
    )
    return jax.shard_map(
        shards,
        mesh=torus,
        in_specs=(P(None, ROW, None, COL_FEAT), P(None, ROW, None)),
        out_specs=(P(None, ROW, None, None, COL, "feat"), P(), P()),
        check_vma=False,
    )
```

profile of v0, /device:TPU:7, one launch (start us, length us, event | category | flops | bytes accessed | tf_op | source)
XLA Modules:
  0.0 444.7 jit_solution(9478531407381892223)
XLA Ops:
  9.1 58.1 %all-gather.7.cloned.1.call-done = bf16[4,1,512,1024]{2,0,1,3:T(4,128)(2,1)} async-done(((bf16[4,1,512,64]{2,0,1,3:T(4,128)(2,1)}), bf16[4,1,512,1024]{2,0,1,3:T(4,128)(2,1)}) %all-gather.7.cloned.1.call-update) | async-done | bytes 4194320 | tf_op jit(solution)/shard_map/all_gather | solution.py:29
  67.3 3.6 slice.185
  70.9 4.3 copy.16
  77.6 3.1 copy.19
  80.8 22.1 %all-gather.1 = bf16[8,1,512]{2,1,0:T(2,128)(2,1)S(1)} all-gather(bf16[1,1,512]{2,1,0:T(2,128)(2,1)S(1)} %slice.203), channel_id=3, replica_groups=mesh['row_0'=2,'row_1'=4,'col_0'=4,'col_1'=2,'feat'=2] {'row_0','row_1'}, dimensions={0}, use_global_device_ids=true | all-gather | bytes 9216 | tf_op jit(solution)/shard_map/all_gather | solution.py:16
  104.2 5.6 %copy.27 = bf16[128,8,4,512]{3,1,2,0:T(8,128)(2,1)} copy(bf16[128,8,4,512]{3,2,1,0:T(4,128)(2,1)} %bitcast.108) | data formatting | bytes 8388608
  109.9 7.7 %copy.20 = bf16[4,1,512,1024]{3,2,0,1:T(8,128)(2,1)} copy(bf16[4,1,512,1024]{2,0,1,3:T(4,128)(2,1)} %all-gather.7.cloned.1.call-done) | data formatting | bytes 8388608 | tf_op jit(solution)/shard_map/all_gather | solution.py:29
  117.6 48.0 %all-gather.9.cloned.1.call-done = bf16[8,1,512,1024]{3,2,1,0:T(8,128)(2,1)} async-done(((bf16[1,1,512,1024]{3,2,1,0:T(8,128)(2,1)}), bf16[8,1,512,1024]{3,2,1,0:T(8,128)(2,1)}) %all-gather.9.cloned.1.call-update) | async-done | bytes 8388624 | tf_op jit(solution)/shard_map/all_gather | solution.py:16
  168.3 6.8 %fusion.14 = f32[2048,512]{1,0:T(8,128)} fusion(bf16[2048,1024]{0,1:T(8,128)(2,1)} %bitcast.112, bf16[8,1,512,1024]{3,2,1,0:T(8,128)(2,1)} %all-gather.9.cloned.1.call-done), kind=kOutput, calls=%fused_computation.33 | convolution fusion | flops 2147483648 | bytes 9437184 | tf_op jit(solution)/shard_map/dot_general | solution.py:47
  175.1 3.1 fusion.21
  179.2 11.7 %cholesky.103 = f32[128,128]{1,0:T(8,128)S(1)} custom-call(f32[128,128]{1,0:T(8,128)S(1)} %cholesky.263), custom_call_target="Cholesky" | custom-call | tf_op jit(solution)/shard_map/jit(cholesky)/cholesky | solution.py:43
  191.0 9.8 %custom-call.31 = f32[1,128,128]{1,2,0:T(8,128)S(1)} custom-call(f32[1,128,128]{2,1,0:T(8,128)S(1)} %get-tuple-element.65), custom_call_target="InvertDiagBlocksLowerTriangular" | custom-call | tf_op jit(solution)/shard_map/jit(cholesky)/cholesky | solution.py:43
  203.4 12.2 %cholesky.215 = f32[128,128]{1,0:T(8,128)S(1)} custom-call(f32[128,128]{1,0:T(8,128)S(1)} %cholesky.267), custom_call_target="Cholesky" | custom-call | tf_op jit(solution)/shard_map/jit(cholesky)/cholesky | solution.py:43
  215.6 9.8 %custom-call.32 = f32[1,128,128]{1,2,0:T(8,128)S(1)} custom-call(f32[1,128,128]{2,1,0:T(8,128)S(1)} %get-tuple-element.62), custom_call_target="InvertDiagBlocksLowerTriangular" | custom-call | tf_op jit(solution)/shard_map/jit(cholesky)/cholesky | solution.py:43
  227.0 11.7 %cholesky.236 = f32[128,128]{1,0:T(8,128)S(1)} custom-call(f32[128,128]{1,0:T(8,128)S(1)} %cholesky.272), custom_call_target="Cholesky" | custom-call | tf_op jit(solution)/shard_map/jit(cholesky)/cholesky | solution.py:43
  238.8 9.8 %custom-call.33 = f32[1,128,128]{1,2,0:T(8,128)S(1)} custom-call(f32[1,128,128]{2,1,0:T(8,128)S(1)} %get-tuple-element.59), custom_call_target="InvertDiagBlocksLowerTriangular" | custom-call | tf_op jit(solution)/shard_map/jit(cholesky)/cholesky | solution.py:43
  250.0 11.9 %cholesky.253 = f32[128,128]{1,0:T(8,128)S(1)} custom-call(f32[128,128]{1,0:T(8,128)S(1)} %convolution_subtract_fusion.5), custom_call_target="Cholesky" | custom-call | tf_op jit(solution)/shard_map/jit(cholesky)/cholesky | solution.py:43
  267.7 13.9 %while.3 = (s32[]{:T(128)}, f32[512,512]{1,0:T(8,128)}, s32[4,2]{0,1:T(2,128)S(1)}, f32[4,128,128]{2,1,0:T(8,128)}, s32[]{:T(128)}) while((s32[]{:T(128)}, f32[512,512]{1,0:T(8,128)}, s32[4,2]{0,1:T(2,128)S(1)}, f32[4,128,128]{2,1,0:T(8,128)}, s32[]{:T(128)}) %tuple.48), condition=%wide.while_cond.2, body=%wide.while_body.2.sunk | while | flops 2 | bytes 132205 | solution.py:44
  268.3 2.9 bitcast_dynamic-update-slice_fusion.2
  275.3 2.9 bitcast_dynamic-update-slice_fusion.2
  281.7 40.1 %custom-call.34 = f32[4,128,128]{1,2,0:T(8,128)S(1)} custom-call(f32[4,128,128]{2,1,0:T(8,128)} %get-tuple-element.34), custom_call_target="InvertDiagBlocksLowerTriangular" | custom-call | tf_op jit(solution)/shard_map/jit(_solve_triangular)/triangular_solve | solution.py:44
  327.7 8.7 %fusion.23 = f32[2048,512]{1,0:T(8,128)S(1)} fusion(f32[2048,512]{1,0:T(8,128)} %get-tuple-element.67, f32[128,512]{1,0:T(8,128)S(1)} %fusion.39, f32[128,512]{1,0:T(8,128)S(1)} %fusion.40, f32[128,512]{1,0:T(8,128)S(1)} %fusion.42, f32[128,512]{1,0:T(8,128)S(1)} %fusion.30), kind=kOutput, calls=%fused_computation.42 | convolution fusion | flops 6443237376 | bytes 9437184 | tf_op jit(solution)/shard_map/dot_general | solution.py:51
  345.4 3.5 fusion.22
  349.0 14.6 %fusion.55 = f32[4,512,4,256]{1,3,0,2:T(8,128)S(1)} fusion(f32[4,512,512,1]{2,1,0,3:T(8,128)S(1)} %bitcast.107, f32[4,256,512,1]{2,1,3,0:T(8,128)S(1)} %bitcast.110), kind=kOutput, calls=%fused_computation.114 | convolution fusion | flops 12884901888 | bytes 14680064 | tf_op jit(solution)/shard_map/lit,mjt->limj/dot_general | solution.py:68
  363.6 9.6 %multiply_reduce_fusion = (f32[]{:T(128)}, f32[4,512,4,256]{1,3,0,2:T(8,128)}) fusion(f32[4,4]{0,1:T(4,128)S(1)} %compare_select_fusion, f32[512,256]{0,1:T(8,128)S(1)} %copy-done.12, f32[4,256]{1,0:T(4,128)S(1)} %bitcast.116, f32[4,4]{0,1:T(4,128)S(1)} %get-tuple-element.70, f32[4,512,4,256]{1,3,0,2:T(8,128)S(1)} %fusion.55, ...), kind=kOutput, calls=%fused_computation.7 | convolution fusion | flops 4313841664 | bytes 25694360 | tf_op jit(solution)/shard_map/lif,mjf->limj/dot_general | solution.py:65
  373.3 4.4 psum.35
  377.7 6.8 %psum.36 = f32[]{:T(128)} all-reduce(f32[]{:T(128)} %psum.35), channel_id=1, replica_groups=mesh['row_0'=2,'row_1'=4,'col_0'=4,'col_1'=2,'feat'=2] {'row_1'}, use_global_device_ids=true, to_apply=%region_10.11 | all-reduce | flops 1 | bytes 8 | tf_op jit(solution)/shard_map/psum | solution.py:20
  384.4 4.5 %gather_fusion = f32[512]{0:T(512)S(1)} fusion(f32[512,512]{1,0:T(8,128)S(1)} %get-tuple-element.53, s32[512]{0:T(512)S(1)} %bitcast.109), kind=kCustom, calls=%fused_computation | custom fusion | bytes 8192 | tf_op jit(solution)/shard_map/jit(diagonal)/cond/branch_0_fun/gather | solution.py:92
  389.0 9.3 %psum.37 = f32[]{:T(128)} all-reduce(f32[]{:T(128)} %psum.36), channel_id=1, replica_groups=mesh['row_0'=2,'row_1'=4,'col_0'=4,'col_1'=2,'feat'=2] {'col_0'}, use_global_device_ids=true, to_apply=%region_11.12 | all-reduce | flops 1 | bytes 8 | tf_op jit(solution)/shard_map/psum | solution.py:20
  398.8 8.8 %psum.38 = f32[]{:T(128)} all-reduce(f32[]{:T(128)} %psum.37), channel_id=1, replica_groups=mesh['row_0'=2,'row_1'=4,'col_0'=4,'col_1'=2,'feat'=2] {'col_1'}, use_global_device_ids=true, to_apply=%region_12.13 | all-reduce | flops 1 | bytes 8 | tf_op jit(solution)/shard_map/psum | solution.py:20
  408.3 5.9 %psum.39 = f32[]{:T(128)} all-reduce(f32[]{:T(128)} %psum.38), channel_id=1, replica_groups=mesh['row_0'=2,'row_1'=4,'col_0'=4,'col_1'=2,'feat'=2] {'feat'}, use_global_device_ids=true, to_apply=%region_13.14 | all-reduce | flops 1 | bytes 8 | tf_op jit(solution)/shard_map/psum | solution.py:20
  414.2 20.7 %copy.22 = f32[4,1,512,4,1,256]{5,4,3,2,1,0:T(1,128)} copy(f32[4,1,512,4,1,256]{2,5,0,3,4,1:T(8,128)} %bitcast.111) | data formatting | bytes 16777216
  (97 shorter events, 41.7 us)
Async XLA Ops:
  7.2 60.1 %all-gather.7.cloned.1.call-start = ((), (), s32[]{:S(2)}) async-start(), calls=%async_computation | async-start | bytes 4456448 | tf_op jit(solution)/shard_map/all_gather | solution.py:29
  9.1 156.5 %all-gather.9.cloned.1.call-start = ((), (), s32[]{:S(2)}) async-start(), calls=%async_computation.1 | async-start | bytes 9437184 | tf_op jit(solution)/shard_map/all_gather | solution.py:16
  75.2 265.6 %all-gather.11.cloned.1.call-start = ((), (), s32[]{:S(2)}) async-start(), calls=%async_computation.2 | async-start | bytes 18874368 | tf_op jit(solution)/shard_map/all_gather | solution.py:39
  77.6 3.2 copy-start.13
  178.2 1.0 copy-start.7
  323.8 12.7 %copy-start.2 = (f32[128,512]{1,0:T(8,128)}, f32[128,512]{1,0:T(8,128)S(1)}, u32[]{:S(2)}) copy-start(f32[128,512]{1,0:T(8,128)S(1)} %fusion.42) | copy-start | bytes 786436
  325.6 10.8 %copy-start.4 = (f32[128,512]{1,0:T(8,128)}, f32[128,512]{1,0:T(8,128)S(1)}, u32[]{:S(2)}) copy-start(f32[128,512]{1,0:T(8,128)S(1)} %fusion.40) | copy-start | bytes 786436
  327.7 8.7 %copy-start.8 = (f32[128,512]{1,0:T(8,128)}, f32[128,512]{1,0:T(8,128)S(1)}, u32[]{:S(2)}) copy-start(f32[128,512]{1,0:T(8,128)S(1)} %fusion.39) | copy-start | bytes 786436
  336.4 2.0 copy-start
  342.6 2.7 copy-start.10
  342.6 2.9 copy-start.3
  342.6 2.9 copy-start.5
  342.6 2.9 copy-start.9
  345.2 3.7 copy-start.1
  348.9 14.6 %copy-start.6 = (bf16[4,1,512,1024]{3,2,0,1:T(8,128)(2,1)S(1)}, bf16[4,1,512,1024]{3,2,0,1:T(8,128)(2,1)}, u32[]{:S(2)}) copy-start(bf16[4,1,512,1024]{3,2,0,1:T(8,128)(2,1)} %copy.20) | copy-start | bytes 12582916
  349.0 14.6 %copy-start.11 = (f32[4,512,256]{1,2,0:T(8,128)S(1)}, f32[4,512,256]{1,2,0:T(8,128)}, u32[]{:S(2)}) copy-start(f32[4,512,256]{1,2,0:T(8,128)} %copy.18) | copy-start | bytes 6291460
  349.0 14.6 %copy-start.12 = (f32[512,256]{0,1:T(8,128)S(1)}, f32[512,256]{0,1:T(8,128)}, u32[]{:S(2)}) copy-start(f32[512,256]{0,1:T(8,128)} %fusion.28) | copy-start | bytes 1572868
Sparse Core Ops, SparseCore 0:
  11.0 56.1 all-gather.6
  75.3 90.1 all-gather.8
  167.2 168.9 all-gather.10
where the time goes:
time: 452 us; the launch traced here: 445 us
  other arithmetic  125 us (28%)
  waiting for transfers between devices  106 us (23%)
  local copies, waits for them, and re-layouts  75.2 us (17%)
  matrix products  59.6 us (13%)
  blocking collectives  57.3 us (13%)
  between operations  20.9 us (5%)
    another operation x14, other arithmetic, shards(): factor = jnp.linalg.cholesky(leading_gram)  79 us
    all_gather x1, waiting for transfers between devices, shards(): row_points = lax.all_gather(points, COL_FEAT, axis=3, tiled=True)[:, 0]  58.1 us
    all_gather x1, waiting for transfers between devices, broadcast(): lax.all_gather(value, axis)  48 us
    another operation x3, other arithmetic, shards(): jax.scipy.linalg.solve_triangular(factor, jnp.eye(tile_size, dtype=jnp.fl...  41.4 us
    psum x5, blocking collectives, over_axes(): return functools.reduce(lax.psum, axes, value)  35.1 us
    unnamed x32, local copies, waits for them, and re-layouts  31.2 us
    all_gather x1, blocking collectives, broadcast(): lax.all_gather(value, axis)  22.1 us
    dot_general x1, matrix products, shards(): jnp.einsum('lit,mjt->limj', row_panel, col_panel, precision=lax.Precision...  14.6 us
  transfers between devices with their start and end apart: 3, of which 2 were waited for; matrix products, arithmetic and copies ran while one was open for 43% of the time, Pallas kernels for 0%

commit v1 on v0

v1 whole, which is shorter than its diff:
```python
import jax
import jax.numpy as jnp
from jax import lax
from jax.experimental import pallas as pl
from jax.experimental.pallas import tpu as pltpu
from jax.sharding import Mesh
from jax.sharding import PartitionSpec as P

F32 = jnp.float32
BF16 = jnp.bfloat16
HIGHEST = lax.Precision.HIGHEST
IDS = pl.DeviceIdType.MESH
AXES = ("x_lo", "y", "z", "core", "x_hi")
ROW = ("x_lo", "y")
COL = ("z", "core")
VMEM = pl.BlockSpec(memory_space=pltpu.VMEM)
ANY = pl.BlockSpec(memory_space=pl.ANY)
VMEM_LIMIT = 60 * 1024 * 1024


def factor_block(block):
    lane = lax.broadcasted_iota(jnp.int32, (8, 128), 1)
    sub = lax.broadcasted_iota(jnp.int32, (8, 128), 0)
    rows, logs = [], jnp.zeros((8, 128), F32)
    top, below = block[:8], block[8:]
    for k in range(16):
        c, n = 8 * k, 120 - 8 * k
        diag = [jnp.broadcast_to(top[:, c + t : c + t + 1], (8, 128)) for t in range(8)]
        here = (lane >= c) & (lane < c + 8)
        top = jnp.where(here, jnp.where(lane - c == sub, 1.0, 0.0), top)
        if n:
            cols = [jnp.broadcast_to(below[:, c + t : c + t + 1], (n, 128)) for t in range(8)]
            wide = lax.broadcasted_iota(jnp.int32, (n, 128), 1)
            below = jnp.where((wide >= c) & (wide < c + 8), 0.0, below)
        pivots = jnp.zeros((8, 128), F32)
        for t in range(8):
            pivot = diag[t][t : t + 1, :]
            inv = 1.0 / pivot
            pivots = jnp.where(sub == t, pivot, pivots)
            factor = jnp.where(sub > t, diag[t] * inv, 0.0)
            row = top[t : t + 1, :]
            ends = [diag[j][t : t + 1, :] for j in range(8)]
            for j in range(t + 1, 8):
                diag[j] = diag[j] - factor * ends[j]
            top = top - factor * row
            if n:
                scaled = cols[t] * inv
                below = below - scaled * row
                for j in range(t + 1, 8):
                    cols[j] = cols[j] - scaled * ends[j]
        rows.append(jnp.where(lane < c + 8, top, 0.0) * lax.rsqrt(pivots))
        logs = logs + jnp.log(pivots)
        if n:
            top, below = below[:8], below[8:]
    return jnp.concatenate(rows, 0), logs


def factor_step(k, w_ref, log_ref):
    n = w_ref.shape[0]
    at = pl.ds(pl.multiple_of(k * 128, 128), 128)
    block, logs = factor_block(w_ref[at, at])
    log_ref[...] += logs
    row_block = lax.broadcasted_iota(jnp.int32, (n, 128), 0) // 128
    col_block = lax.broadcasted_iota(jnp.int32, (128, n), 1) // 128
    all_block = lax.broadcasted_iota(jnp.int32, (n, n), 1) // 128
    lead = jnp.dot(block, w_ref[at, :], precision=HIGHEST)
    lead = jnp.where(col_block == k, jnp.concatenate([block] * (n // 128), 1), lead)
    left = lax.dot_general(w_ref[:, at], block, (((1,), (1,)), ((), ())), precision=HIGHEST)
    left = jnp.where(row_block > k, left, 0.0)
    rest = jnp.where(all_block == k, 0.0, w_ref[...])
    w_ref[...] = rest - jnp.dot(left, lead, precision=HIGHEST)
    w_ref[at, :] = lead


def remote(src, dst, send, recv, to):
    return pltpu.make_async_remote_copy(
        src_ref=src, dst_ref=dst, send_sem=send, recv_sem=recv, device_id=to, device_id_type=IDS
    )


def gather_kernel(
    x_ref, s_ref,
    rows_out, cols_out, lead_out, leadt_out, w_ref, log_ref,
    lead, rows, cols, noise,
    local_sem, own_sem, out_sem, lead_send, lead_recv, noise_send, noise_recv, line_send, line_recv,
    swap_send, swap_recv, row_send, row_recv, rswap_send, rswap_recv, spread_send, spread_recv, col_send, col_recv,
):
    a, b, z, k, h = (lax.axis_index(name) for name in AXES)
    q_line = z * 2 + h
    q_plane = b * 2 + a
    partner = {"core": 1 - k}

    def plane(d):
        return {"x_lo": (a + d // 4) % 2, "y": (b + d % 4) % 4}

    def line(d):
        return {"x_hi": (h + d // 4) % 2, "z": (z + d % 4) % 4}

    row_group = a * 4 + b
    to_z, to_k = row_group // 2, row_group % 2
    col_group = z * 2 + k
    from_a, from_b = col_group // 4, col_group % 4

    def spread_to(f):
        return {"x_lo": h, "y": z, "z": to_z, "core": to_k, "x_hi": f}

    def spread_self(f):
        return (a == h) & (b == z) & (z == to_z) & (k == to_k) & (h == f)

    def spread_from(kk):
        return {"x_lo": from_a, "y": from_b, "z": b, "core": kk, "x_hi": a}

    def from_self(kk):
        return (a == from_a) & (b == from_b) & (z == b) & (k == kk) & (h == a)

    own_row = pltpu.make_async_copy(x_ref, rows.at[q_line, k], own_sem)
    own_row.start()

    barrier = pltpu.get_barrier_semaphore()
    for d in range(1, 8):
        pl.semaphore_signal(barrier, inc=1, device_id=plane(d), device_id_type=IDS)
        pl.semaphore_signal(barrier, inc=1, device_id=line(d), device_id_type=IDS)
    pl.semaphore_signal(barrier, inc=1, device_id=partner, device_id_type=IDS)
    for i in range(2):
        @pl.when(jnp.logical_not(spread_self(i)))
        def _():
            pl.semaphore_signal(barrier, inc=1, device_id=spread_to(i), device_id_type=IDS)

        @pl.when(jnp.logical_not(from_self(i)))
        def _():
            pl.semaphore_signal(barrier, inc=1, device_id=spread_from(i), device_id_type=IDS)

    selfish = spread_self(0) | spread_self(1)

    @pl.when(selfish)
    def _():
        pl.semaphore_wait(barrier, 17)

    @pl.when(jnp.logical_not(selfish))
    def _():
        pl.semaphore_wait(barrier, 19)

    source = (a == 0) & (b == 0)

    @pl.when(source)
    def _():
        for d in range(1, 8):
            remote(x_ref.at[0], lead.at[q_line, k], lead_send.at[d - 1], lead_recv, plane(d)).start()
            remote(s_ref.at[0], noise, noise_send.at[d - 1], noise_recv, plane(d)).start()
        here = pltpu.make_async_copy(x_ref.at[0], lead.at[q_line, k], local_sem.at[0])
        there = pltpu.make_async_copy(s_ref.at[0], noise, local_sem.at[1])
        here.start()
        there.start()
        here.wait()
        there.wait()

    @pl.when(jnp.logical_not(source))
    def _():
        pltpu.make_async_copy(x_ref.at[0], lead.at[q_line, k], lead_recv).wait()
        pltpu.make_async_copy(s_ref.at[0], noise, noise_recv).wait()

    for d in range(1, 8):
        remote(
            lead.at[q_line, k], lead.at[q_line, k], line_send.at[d - 1], line_recv.at[q_line], line(d)
        ).start()
    for d in range(1, 8):
        q = ((z + d % 4) % 4) * 2 + (h + d // 4) % 2
        pltpu.make_async_copy(lead.at[q, k], lead.at[q, k], line_recv.at[q]).wait()
    swap = remote(lead.at[:, k], lead.at[:, k], swap_send, swap_recv, partner)
    swap.start()

    def row_piece(q, slot, to):
        return remote(rows.at[q, k], rows.at[q, k], row_send.at[slot], row_recv.at[q], to)

    def row_wait(q):
        pltpu.make_async_copy(rows.at[q, k], rows.at[q, k], row_recv.at[q]).wait()

    def col_piece(q, slot, to):
        return remote(cols.at[q], cols.at[q], col_send.at[slot], col_recv.at[q], to)

    def col_wait(q):
        pltpu.make_async_copy(cols.at[q], cols.at[q], col_recv.at[q]).wait()

    up_z, down_z = {"z": (z + 1) % 4}, {"z": (z + 3) % 4}
    up_y, down_y = {"y": (b + 1) % 4}, {"y": (b + 3) % 4}
    q_pair = z * 2 + 1 - h
    q_cross = b * 2 + 1 - a

    own_row.wait()
    row_piece(q_line, 0, {"x_hi": 1 - h}).start()
    row_piece(q_line, 1, up_z).start()
    row_piece(q_line, 2, down_z).start()
    for f in range(2):
        half = x_ref.at[:, :, f * 256 : f * 256 + 256]
        place = cols.at[q_line, k]

        @pl.when(spread_self(f))
        def _():
            pltpu.make_async_copy(half, place, spread_recv.at[k]).start()

        @pl.when(jnp.logical_not(spread_self(f)))
        def _():
            remote(half, place, spread_send.at[f], spread_recv.at[k], spread_to(f)).start()

    pltpu.make_async_copy(lead.at[:, k], lead.at[:, k], swap_recv).wait()
    for q in range(8):
        for kk in range(2):
            part = (q * 2 + kk) * 64
            leadt_out[part : part + 64, :] = lead[q, kk]
    lead_out[...] = leadt_out[...].T
    diag = lax.broadcasted_iota(jnp.int32, (128, 128), 0) == lax.broadcasted_iota(jnp.int32, (128, 128), 1)
    for i in range(4):
        block = slice(i * 128, i * 128 + 128)
        w_ref[block, :] = jnp.dot(lead_out[block, :], leadt_out[...], preferred_element_type=F32)
        w_ref[block, block] += jnp.where(diag, noise[i : i + 1, :], 0.0)
    log_ref[...] = jnp.zeros_like(log_ref)

    def step(i, carry):
        factor_step(i, w_ref, log_ref)

        @pl.when(i == 0)
        def _():
            for kk in range(2):
                q = q_plane
                pltpu.make_async_copy(cols.at[q, kk], cols.at[q, kk], spread_recv.at[kk]).wait()
            col_piece(q_plane, 0, {"x_lo": 1 - a}).start()
            col_piece(q_plane, 1, up_y).start()
            col_piece(q_plane, 2, down_y).start()
            row_wait(q_pair)
            row_piece(q_pair, 3, up_z).start()
            row_piece(q_pair, 4, down_z).start()

        @pl.when(i == 1)
        def _():
            col_wait(q_cross)
            col_piece(q_cross, 3, up_y).start()
            col_piece(q_cross, 4, down_y).start()
            for j in range(2):
                row_wait(((z + 3) % 4) * 2 + j)
                row_wait(((z + 1) % 4) * 2 + j)
            row_piece(((z + 3) % 4) * 2, 5, up_z).start()
            row_piece(((z + 1) % 4) * 2 + 1, 6, down_z).start()

        @pl.when(i == 2)
        def _():
            for j in range(2):
                col_wait(((b + 3) % 4) * 2 + j)
                col_wait(((b + 1) % 4) * 2 + j)
            col_piece(((b + 3) % 4) * 2, 5, up_y).start()
            col_piece(((b + 1) % 4) * 2 + 1, 6, down_y).start()
            row_wait(((z + 2) % 4) * 2)
            row_wait(((z + 2) % 4) * 2 + 1)
            remote(rows.at[:, k], rows.at[:, k], rswap_send, rswap_recv, partner).start()

        return carry

    lax.fori_loop(0, 4, step, 0)
    n = w_ref.shape[0]
    lower = lax.broadcasted_iota(jnp.int32, (n, n), 0) >= lax.broadcasted_iota(jnp.int32, (n, n), 1)
    w_ref[...] = jnp.where(lower, w_ref[...], 0.0)

    col_wait(((b + 2) % 4) * 2)
    col_wait(((b + 2) % 4) * 2 + 1)
    put_cols = pltpu.make_async_copy(cols, cols_out, out_sem.at[0])
    put_cols.start()
    pltpu.make_async_copy(rows.at[:, k], rows.at[:, k], rswap_recv).wait()
    put_rows = pltpu.make_async_copy(rows, rows_out, out_sem.at[1])
    put_rows.start()

    @pl.when(source)
    def _():
        for d in range(1, 8):
            remote(x_ref.at[0], lead.at[q_line, k], lead_send.at[d - 1], lead_recv, plane(d)).wait_send()
            remote(s_ref.at[0], noise, noise_send.at[d - 1], noise_recv, plane(d)).wait_send()

    for d in range(1, 8):
        remote(
            lead.at[q_line, k], lead.at[q_line, k], line_send.at[d - 1], line_recv.at[q_line], line(d)
        ).wait_send()
    swap.wait_send()
    for i in range(7):
        row_piece(q_line, i, up_z).wait_send()
        col_piece(q_plane, i, up_y).wait_send()
    for f in range(2):
        @pl.when(jnp.logical_not(spread_self(f)))
        def _():
            half = x_ref.at[:, :, f * 256 : f * 256 + 256]
            remote(half, cols.at[q_line, k], spread_send.at[f], spread_recv.at[k], spread_to(f)).wait_send()

    remote(rows.at[:, k], rows.at[:, k], rswap_send, rswap_recv, partner).wait_send()
    put_cols.wait()
    put_rows.wait()


def gather(x, s):
    dma = pltpu.SemaphoreType.DMA
    return pl.pallas_call(
        gather_kernel,
        out_shape=(
            jax.ShapeDtypeStruct((8, 2, 4, 64, 512), BF16),
            jax.ShapeDtypeStruct((8, 2, 4, 64, 256), BF16),
            jax.ShapeDtypeStruct((512, 1024), BF16),
            jax.ShapeDtypeStruct((1024, 512), BF16),
            jax.ShapeDtypeStruct((512, 512), F32),
            jax.ShapeDtypeStruct((8, 128), F32),
        ),
        in_specs=[ANY, ANY],
        out_specs=(ANY, ANY, VMEM, VMEM, VMEM, VMEM),
        scratch_shapes=[
            pltpu.VMEM((8, 2, 64, 512), BF16),
            pltpu.VMEM((8, 2, 4, 64, 512), BF16),
            pltpu.VMEM((8, 2, 4, 64, 256), BF16),
            pltpu.VMEM((4, 128), F32),
            dma((2,)), dma, dma((2,)),
            dma((7,)), dma, dma((7,)), dma, dma((7,)), dma((8,)),
            dma, dma, dma((7,)), dma((8,)), dma, dma, dma((2,)), dma((2,)), dma((7,)), dma((8,)),
        ],
        compiler_params=pltpu.CompilerParams(
            collective_id=0, has_side_effects=True, vmem_limit_bytes=VMEM_LIMIT
        ),
        name="gather_factor",
    )(x, s)


def split(value):
    high = value.astype(BF16)
    return high, (value - high.astype(F32)).astype(BF16)


def dot(left, right):
    return jnp.dot(left, right, preferred_element_type=F32)


def schur_kernel(
    rows_ref, cols_ref, lead_ref, leadt_ref, w_ref, s_ref,
    out_ref, trace_ref,
    wt, points, high, low, col_high, col_low,
):
    l = pl.program_id(0)
    r = lax.axis_index(ROW)
    c = lax.axis_index(COL)
    f = lax.axis_index("x_hi")
    diag = lax.broadcasted_iota(jnp.int32, (512, 512), 0) == lax.broadcasted_iota(jnp.int32, (512, 512), 1)

    @pl.when(l == 0)
    def _():
        wt[...] = w_ref[...].T
        trace_ref[...] = jnp.zeros_like(trace_ref)
        for m in range(4):
            first = dot(lead_ref[...], cols_ref[:, :, m].reshape(1024, 256))
            col_high[m], col_low[m] = split(jnp.dot(w_ref[...], first, precision=HIGHEST))

    points[...] = rows_ref[...].reshape(1024, 512).T
    first = dot(points[...], leadt_ref[...])
    corner = (l == 0) & (r == 0)
    noise = s_ref[0]
    first = first + jnp.where(diag & corner, noise, 0.0)
    panel = jnp.dot(first, wt[...], precision=HIGHEST)
    high[...], low[...] = split(panel)

    @pl.when(jnp.logical_not(corner))
    def _():
        given = points[...].astype(F32)
        total = jnp.sum(given * given, axis=0, keepdims=True)
        minus = jnp.sum(panel * panel, axis=0, keepdims=True)
        total = total[:, :512] + total[:, 512:] + noise - minus
        trace_ref[...] += total

    near = lax.broadcasted_iota(jnp.int32, (512, 256), 0) == lax.broadcasted_iota(jnp.int32, (512, 256), 1) + f * 256
    for m in range(4):
        def put(value):
            for half in range(2):
                out_ref[pl.ds(m * 2 + half, 512, stride=8), :] = value[:, half * 128 : half * 128 + 128]

        is_panel = (c == 0) & (m == 0)
        inside = (l > m) | ((l == m) & (r >= c))

        @pl.when(is_panel)
        def _():
            for half in range(2):
                at = pl.ds(pl.multiple_of(f * 256 + half * 128, 128), 128)
                out_ref[pl.ds(m * 2 + half, 512, stride=8), :] = high[:, at].astype(F32) + low[:, at].astype(F32)

        @pl.when(inside & jnp.logical_not(is_panel))
        def _():
            value = dot(points[...], cols_ref[:, :, m].reshape(1024, 256))
            value = value - dot(high[...], col_high[m])
            value = value - dot(high[...], col_low[m])
            value = value - dot(low[...], col_high[m])
            here = noise[:, :256] * (f == 0).astype(F32) + noise[:, 256:] * (f == 1).astype(F32)
            put(value + jnp.where(near & (l == m) & (r == c), here, 0.0))

        @pl.when(jnp.logical_not(inside))
        def _():
            put(jnp.zeros((512, 256), F32))


def schur(rows, cols, lead, leadt, w, s):
    return pl.pallas_call(
        schur_kernel,
        grid=(4,),
        out_shape=(
            jax.ShapeDtypeStruct((4 * 512 * 8, 128), F32),
            jax.ShapeDtypeStruct((1, 512), F32),
        ),
        in_specs=[
            pl.BlockSpec((8, 2, None, 64, 512), lambda l: (0, 0, l, 0, 0)),
            VMEM, VMEM, VMEM, VMEM,
            pl.BlockSpec((1, 1, 512), lambda l: (l, 0, 0)),
        ],
        out_specs=(
            pl.BlockSpec((512 * 8, 128), lambda l: (l, 0)),
            pl.BlockSpec((1, 512), lambda l: (0, 0)),
        ),
        scratch_shapes=[
            pltpu.VMEM((512, 512), F32),
            pltpu.VMEM((512, 1024), BF16),
            pltpu.VMEM((512, 512), BF16),
            pltpu.VMEM((512, 512), BF16),
            pltpu.VMEM((4, 512, 256), BF16),
            pltpu.VMEM((4, 512, 256), BF16),
        ],
        compiler_params=pltpu.CompilerParams(vmem_limit_bytes=VMEM_LIMIT),
        name="schur",
    )(rows, cols, lead, leadt, w, s)


def shards(points, point_noise):
    x = jnp.swapaxes(points[:, 0], 1, 2)
    s = point_noise.reshape(4, 512)
    rows, cols, lead, leadt, w, logs = gather(x, s.reshape(4, 4, 128))
    out, trace = schur(rows, cols, lead, leadt, w, s.reshape(4, 1, 512))
    total = lax.psum(jnp.sum(trace), ROW)
    count = 32 * 512 - 512
    return out.reshape(4, 1, 512, 4, 1, 256), total / count, jnp.sum(logs[:, 0])


def solution(mesh):
    torus = Mesh(mesh.devices.reshape(2, 4, 4, 2, mesh.shape["feat"]), AXES)
    return jax.shard_map(
        shards,
        mesh=torus,
        in_specs=(P(None, ROW, None, ("z", "core", "x_hi")), P(None, ROW, None)),
        out_specs=(P(None, ROW, None, None, COL, "x_hi"), P(), P()),
        check_vma=False,
    )
```

time: 452 us -> 121 us (0.27)
  the two profiles are of different devices: /device:TPU:7 before, /device:TPU:38 now
where the time goes in v1:
time: 121 us
  Pallas kernels  95.9 us (79%)
  blocking collectives  20 us (17%)
  other arithmetic  2.58 us (2%)
  between operations  2.42 us (2%)
    pallas_call x1, Pallas kernels, gather(): pl.pallas_call(gather_kernel, out_shape=(jax.ShapeDtypeStruct((8, 2, 4, 6...  66.8 us
    pallas_call x1, Pallas kernels, schur(): pl.pallas_call(schur_kernel, grid=(4,), out_shape=(jax.ShapeDtypeStruct((...  29.1 us
    psum x1, blocking collectives, shards(): total = lax.psum(jnp.sum(trace), ROW)  20 us

profile of v1, /device:TPU:38, one launch (start us, length us, event | category | flops | bytes accessed | tf_op | source)
XLA Modules:
  0.0 120.9 jit_solution(17446527646187758838)
XLA Ops:
  0.6 66.8 %gather_factor.1 = (bf16[8,2,4,64,512]{4,3,2,1,0:T(8,128)(2,1)}, bf16[8,2,4,64,256]{4,3,2,1,0:T(8,128)(2,1)}, bf16[512,1024]{1,0:T(8,128)(2,1)}, bf16[1024,512]{...) custom-call(bf16[4,64,512]{2,1,0:T(8,128)(2,1)} %bitcast.5, f32[4,4,128]{2,1,0:T(4,128)} %bitcast.6), custom_call_target="tpu_custom_call" | custom-call | tf_op jit(solution)/shard_map/gather_factor/pallas_call | solution.py:297
  67.4 1.3 %slice_reduce_fusion = f32[]{:T(128)} fusion(f32[8,128]{1,0:T(8,128)} %get-tuple-element.18), kind=kLoop, calls=%fused_computation | loop fusion | flops 7 | bytes 36 | tf_op jit(solution)/shard_map/reduce_sum | solution.py:435
  68.7 29.1 %schur.1 = (f32[16384,128]{1,0:T(8,128)}, f32[1,512]{1,0:T(1,128)}) custom-call(bf16[8,2,4,64,512]{4,3,2,1,0:T(8,128)(2,1)} %get-tuple-element.11.rows_ref, bf16[8,2,4,64,256]{4,3,2,1,0:T(8,128)(2,1)} %get-tuple-element.12.cols_ref, bf16[512,1024]{1,0:T(8,128)(2,1)} %get-tuple-element.13.lead_ref, bf16[1024,512]{1,0:T(8,128)(2,1)} %get-tuple-element.14.leadt_ref, ...), custom_call_target="tpu_custom_call" | custom-call | tf_op jit(solution)/shard_map/schur/pallas_call | solution.py:399
  97.8 1.3 %reduce_sum.18 = f32[]{:T(128)} reduce(f32[1,512]{1,0:T(1,128)} %get-tuple-element.17, f32[]{:T(128)} %constant.1.clone.1), dimensions={0,1}, to_apply=%region_0.0 | reduce | flops 511 | bytes 2056 | tf_op jit(solution)/shard_map/reduce_sum | solution.py:433
  99.1 20.0 %psum.7 = f32[]{:T(128)} all-reduce(f32[]{:T(128)} %reduce_sum.18), channel_id=1, replica_groups=mesh['x_lo'=2,'y'=4,'z'=4,'core'=2,'x_hi'=2] {'x_lo','y'}, use_global_device_ids=true, to_apply=%region_1.0 | all-reduce | flops 1 | bytes 8 | tf_op jit(solution)/shard_map/psum | solution.py:433

commit v2 on v1

v2 whole, which is shorter than its diff:
```python
import jax
import jax.numpy as jnp
from jax import lax
from jax.experimental import pallas as pl
from jax.experimental.pallas import tpu as pltpu
from jax.sharding import Mesh
from jax.sharding import PartitionSpec as P

F32 = jnp.float32
BF16 = jnp.bfloat16
HIGHEST = lax.Precision.HIGHEST
IDS = pl.DeviceIdType.MESH
AXES = ("x_lo", "y", "z", "core", "x_hi")
ROW = ("x_lo", "y")
COL = ("z", "core")
VMEM = pl.BlockSpec(memory_space=pltpu.VMEM)
ANY = pl.BlockSpec(memory_space=pl.ANY)
VMEM_LIMIT = 60 * 1024 * 1024


def factor_block(block):
    lane = lax.broadcasted_iota(jnp.int32, (8, 128), 1)
    sub = lax.broadcasted_iota(jnp.int32, (8, 128), 0)
    rows, logs = [], jnp.zeros((8, 128), F32)
    top, below = block[:8], block[8:]
    for k in range(16):
        c, n = 8 * k, 120 - 8 * k
        diag = [jnp.broadcast_to(top[:, c + t : c + t + 1], (8, 128)) for t in range(8)]
        here = (lane >= c) & (lane < c + 8)
        top = jnp.where(here, jnp.where(lane - c == sub, 1.0, 0.0), top)
        if n:
            cols = [jnp.broadcast_to(below[:, c + t : c + t + 1], (n, 128)) for t in range(8)]
            wide = lax.broadcasted_iota(jnp.int32, (n, 128), 1)
            below = jnp.where((wide >= c) & (wide < c + 8), 0.0, below)
        pivots = jnp.zeros((8, 128), F32)
        for t in range(8):
            pivot = diag[t][t : t + 1, :]
            inv = 1.0 / pivot
            pivots = jnp.where(sub == t, pivot, pivots)
            factor = jnp.where(sub > t, diag[t] * inv, 0.0)
            row = top[t : t + 1, :]
            ends = [diag[j][t : t + 1, :] for j in range(8)]
            for j in range(t + 1, 8):
                diag[j] = diag[j] - factor * ends[j]
            top = top - factor * row
            if n:
                scaled = cols[t] * inv
                below = below - scaled * row
                for j in range(t + 1, 8):
                    cols[j] = cols[j] - scaled * ends[j]
        rows.append(jnp.where(lane < c + 8, top, 0.0) * lax.rsqrt(pivots))
        logs = logs + jnp.log(pivots)
        if n:
            top, below = below[:8], below[8:]
    return jnp.concatenate(rows, 0), logs


def factor_step(k, w_ref, log_ref, between):
    n = w_ref.shape[0]
    at = pl.ds(pl.multiple_of(k * 128, 128), 128)
    block, logs = factor_block(w_ref[at, at])
    log_ref[...] += logs
    between()
    row_block = lax.broadcasted_iota(jnp.int32, (n, 128), 0) // 128
    col_block = lax.broadcasted_iota(jnp.int32, (128, n), 1) // 128
    all_block = lax.broadcasted_iota(jnp.int32, (n, n), 1) // 128
    lead = jnp.dot(block, w_ref[at, :], precision=HIGHEST)
    lead = jnp.where(col_block == k, jnp.concatenate([block] * (n // 128), 1), lead)
    left = lax.dot_general(w_ref[:, at], block, (((1,), (1,)), ((), ())), precision=HIGHEST)
    left = jnp.where(row_block > k, left, 0.0)
    rest = jnp.where(all_block == k, 0.0, w_ref[...])
    w_ref[...] = rest - jnp.dot(left, lead, precision=HIGHEST)
    w_ref[at, :] = lead


def remote(src, dst, send, recv, to):
    return pltpu.make_async_remote_copy(
        src_ref=src, dst_ref=dst, send_sem=send, recv_sem=recv, device_id=to, device_id_type=IDS
    )


def gather_kernel(
    x_ref, s_ref,
    rows_out, cols_out, lead_out, leadt_out, w_ref, log_ref,
    lead, rows, cols, noise,
    own_sem, row_out, col_out, lead_send, lead_recv, noise_send, noise_recv, line_send, line_recv,
    swap_send, swap_recv, row_send, row_recv, rswap_send, rswap_recv, spread_send, spread_recv, col_send, col_recv,
):
    a, b, z, k, h = (lax.axis_index(name) for name in AXES)
    q_line = z * 2 + h
    partner = {"core": 1 - k}

    def plane(d):
        return {"x_lo": (a + d // 4) % 2, "y": (b + d % 4) % 4}

    def line(d):
        return {"x_hi": (h + d // 4) % 2, "z": (z + d % 4) % 4}

    row_group = a * 4 + b
    to_z, to_k = row_group // 2, row_group % 2
    to_a, to_b = (a + h) % 2, (b + z) % 4
    col_group = z * 2 + k
    from_a, from_b = col_group // 4, col_group % 4

    def spread_to(f):
        return {"x_lo": to_a, "y": to_b, "z": to_z, "core": to_k, "x_hi": f}

    def spread_self(f):
        return (a == to_a) & (b == to_b) & (z == to_z) & (k == to_k) & (h == f)

    def spread_from(kk):
        return {"x_lo": from_a, "y": from_b, "z": (b + 4 - from_b) % 4, "core": kk, "x_hi": (a + from_a) % 2}

    def from_self(kk):
        return (
            (a == from_a) & (b == from_b) & (z == (b + 4 - from_b) % 4) & (k == kk) & (h == (a + from_a) % 2)
        )

    def q_at(da, db):
        return ((b + db + 4 - from_b) % 4) * 2 + (a + da + from_a) % 2

    def q_on(j, db):
        return ((b + db + 4 - from_b) % 4) * 2 + (j + from_a) % 2

    q_plane = q_at(0, 0)

    own_row = pltpu.make_async_copy(x_ref, rows.at[q_line, k], own_sem)
    own_row.start()

    barrier = pltpu.get_barrier_semaphore()
    for d in range(1, 8):
        pl.semaphore_signal(barrier, inc=1, device_id=plane(d), device_id_type=IDS)
        pl.semaphore_signal(barrier, inc=1, device_id=line(d), device_id_type=IDS)
    pl.semaphore_signal(barrier, inc=1, device_id=partner, device_id_type=IDS)
    for i in range(2):
        @pl.when(jnp.logical_not(spread_self(i)))
        def _():
            pl.semaphore_signal(barrier, inc=1, device_id=spread_to(i), device_id_type=IDS)

        @pl.when(jnp.logical_not(from_self(i)))
        def _():
            pl.semaphore_signal(barrier, inc=1, device_id=spread_from(i), device_id_type=IDS)

    selfish = spread_self(0) | spread_self(1)

    @pl.when(selfish)
    def _():
        pl.semaphore_wait(barrier, 17)

    @pl.when(jnp.logical_not(selfish))
    def _():
        pl.semaphore_wait(barrier, 19)

    def row_piece(q, slot, to):
        src = x_ref if slot < 3 else rows.at[q, k]
        return remote(src, rows.at[q, k], row_send.at[slot], row_recv.at[q], to)

    def row_wait(q):
        pltpu.make_async_copy(rows.at[q, k], rows.at[q, k], row_recv.at[q]).wait()

    def col_piece(q, slot, to):
        return remote(cols.at[q], cols.at[q], col_send.at[slot], col_recv.at[q], to)

    def col_wait(q):
        pltpu.make_async_copy(cols.at[q], cols.at[q], col_recv.at[q]).wait()

    def put_col(q, slot):
        return pltpu.make_async_copy(cols.at[q], cols_out.at[q], col_out.at[slot])

    def put_row(kk, slot):
        return pltpu.make_async_copy(rows.at[:, kk], rows_out.at[:, kk], row_out.at[slot])

    up_z, down_z = {"z": (z + 1) % 4}, {"z": (z + 3) % 4}
    up_y, down_y = {"y": (b + 1) % 4}, {"y": (b + 3) % 4}
    q_pair = z * 2 + 1 - h
    q_cross = q_at(1, 0)

    root = b == 0
    source = root & (a == 0)

    def lead_part(i):
        return pl.ds(i * 32, 32)

    def lead_piece(i, d, to):
        part = lead_part(i)
        dst = lead.at[q_line, k, part]
        return remote(dst, dst, lead_send.at[i, d], lead_recv.at[i], to)

    def noise_piece(d, to):
        return remote(noise, noise, noise_send.at[d], noise_recv, to)

    @pl.when(source)
    def _():
        for i in range(2):
            pltpu.make_async_copy(x_ref.at[0, lead_part(i)], lead.at[q_line, k, lead_part(i)], lead_recv.at[i]).start()
        pltpu.make_async_copy(s_ref.at[0], noise, noise_recv).start()

    def lead_wait(i):
        part = lead.at[q_line, k, lead_part(i)]
        pltpu.make_async_copy(part, part, lead_recv.at[i]).wait()

        @pl.when(source)
        def _():
            lead_piece(i, 0, {"x_lo": 1 - a}).start()

        @pl.when(root)
        def _():
            for d in range(1, 4):
                lead_piece(i, d, {"y": (b + d) % 4}).start()

    def spread():
        for f in range(2):
            half = x_ref.at[:, :, f * 256 : f * 256 + 256]
            place = cols.at[q_line, k]

            @pl.when(spread_self(f))
            def _():
                pltpu.make_async_copy(half, place, spread_recv.at[k]).start()

            @pl.when(jnp.logical_not(spread_self(f)))
            def _():
                remote(half, place, spread_send.at[f], spread_recv.at[k], spread_to(f)).start()

    pl.when(jnp.logical_not(root))(spread)

    def line_piece(i, d):
        part = lead.at[q_line, k, lead_part(i)]
        return remote(part, part, line_send.at[i, d - 1], line_recv.at[i, q_line], line(d))

    for i in range(2):
        lead_wait(i)
        for d in range(1, 8):
            line_piece(i, d).start()
    pl.when(root)(spread)
    pltpu.make_async_copy(noise, noise, noise_recv).wait()

    @pl.when(source)
    def _():
        noise_piece(0, {"x_lo": 1 - a}).start()

    @pl.when(root)
    def _():
        for d in range(1, 4):
            noise_piece(d, {"y": (b + d) % 4}).start()

    for kk in range(2):
        pltpu.make_async_copy(cols.at[q_plane, kk], cols.at[q_plane, kk], spread_recv.at[kk]).wait()
    col_piece(q_plane, 1, up_y).start()
    col_piece(q_plane, 2, down_y).start()
    col_piece(q_plane, 0, {"x_lo": 1 - a}).start()

    for d in range(1, 8):
        q = ((z + d % 4) % 4) * 2 + (h + d // 4) % 2
        for i in range(2):
            part = lead.at[q, k, lead_part(i)]
            pltpu.make_async_copy(part, part, line_recv.at[i, q]).wait()
    swap = remote(lead.at[:, k], lead.at[:, k], swap_send, swap_recv, partner)
    swap.start()
    row_piece(q_line, 0, {"x_hi": 1 - h}).start()
    row_piece(q_line, 1, up_z).start()
    row_piece(q_line, 2, down_z).start()
    pltpu.make_async_copy(lead.at[:, k], lead.at[:, k], swap_recv).wait()
    for q in range(8):
        for kk in range(2):
            part = (q * 2 + kk) * 64
            leadt_out[part : part + 64, :] = lead[q, kk]
    lead_out[...] = leadt_out[...].T
    diag = lax.broadcasted_iota(jnp.int32, (128, 128), 0) == lax.broadcasted_iota(jnp.int32, (128, 128), 1)
    for i in range(4):
        block = slice(i * 128, i * 128 + 128)
        w_ref[block, :] = jnp.dot(lead_out[block, :], leadt_out[...], preferred_element_type=F32)
        w_ref[block, block] += jnp.where(diag, noise[i : i + 1, :], 0.0)
    log_ref[...] = jnp.zeros_like(log_ref)

    col_wait(q_cross)
    col_piece(q_cross, 3, up_y).start()
    col_piece(q_cross, 4, down_y).start()
    own_row.wait()

    def events(step):
        if step == 0:
            row_wait(q_pair)
            row_piece(q_pair, 3, up_z).start()
            row_piece(q_pair, 4, down_z).start()
        if step == 1:
            for j in range(2):
                col_wait(q_on(j, 3))
                col_wait(q_on(j, 1))
            col_piece(q_on(0, 3), 5, up_y).start()
            col_piece(q_on(1, 1), 6, down_y).start()
            for j in range(2):
                for d in range(3):
                    put_col(q_on(j, d + 3), d * 2 + j).start()
        if step == 3:
            for j in range(2):
                row_wait(((z + 3) % 4) * 2 + j)
                row_wait(((z + 1) % 4) * 2 + j)
            row_piece(((z + 3) % 4) * 2, 5, up_z).start()
            row_piece(((z + 1) % 4) * 2 + 1, 6, down_z).start()
        if step == 4:
            for j in range(2):
                col_wait(q_on(j, 2))
                put_col(q_on(j, 2), 6 + j).start()
        if step == 6:
            row_wait(((z + 2) % 4) * 2)
            row_wait(((z + 2) % 4) * 2 + 1)
            remote(rows.at[:, k], rows.at[:, k], rswap_send, rswap_recv, partner).start()
            put_row(k, 0).start()

    def step(i, carry):
        def between():
            for e in (0, 2, 3):
                pl.when(i == e)(lambda e=e: events(2 * e))

        factor_step(i, w_ref, log_ref, between)
        for e in (0, 1):
            pl.when(i == e)(lambda e=e: events(2 * e + 1))
        return carry

    lax.fori_loop(0, 4, step, 0)
    n = w_ref.shape[0]
    lower = lax.broadcasted_iota(jnp.int32, (n, n), 0) >= lax.broadcasted_iota(jnp.int32, (n, n), 1)
    w_ref[...] = jnp.where(lower, w_ref[...], 0.0)

    pltpu.make_async_copy(rows.at[:, k], rows.at[:, k], rswap_recv).wait()
    put_row(1 - k, 1).start()

    for i in range(2):
        @pl.when(source)
        def _():
            lead_piece(i, 0, partner).wait_send()

        @pl.when(root)
        def _():
            for d in range(1, 4):
                lead_piece(i, d, partner).wait_send()

        for d in range(1, 8):
            line_piece(i, d).wait_send()

    @pl.when(source)
    def _():
        noise_piece(0, partner).wait_send()

    @pl.when(root)
    def _():
        for d in range(1, 4):
            noise_piece(d, partner).wait_send()

    swap.wait_send()
    for i in range(7):
        row_piece(q_line, i, up_z).wait_send()
        col_piece(q_plane, i, up_y).wait_send()
    for f in range(2):
        @pl.when(jnp.logical_not(spread_self(f)))
        def _():
            half = x_ref.at[:, :, f * 256 : f * 256 + 256]
            remote(half, cols.at[q_line, k], spread_send.at[f], spread_recv.at[k], spread_to(f)).wait_send()

    remote(rows.at[:, k], rows.at[:, k], rswap_send, rswap_recv, partner).wait_send()
    for j in range(2):
        put_row(k, j).wait()
    for j in range(8):
        put_col(q_plane, j).wait()


def gather(x, s):
    dma = pltpu.SemaphoreType.DMA
    return pl.pallas_call(
        gather_kernel,
        out_shape=(
            jax.ShapeDtypeStruct((8, 2, 4, 64, 512), BF16),
            jax.ShapeDtypeStruct((8, 2, 4, 64, 256), BF16),
            jax.ShapeDtypeStruct((512, 1024), BF16),
            jax.ShapeDtypeStruct((1024, 512), BF16),
            jax.ShapeDtypeStruct((512, 512), F32),
            jax.ShapeDtypeStruct((8, 128), F32),
        ),
        in_specs=[ANY, ANY],
        out_specs=(ANY, ANY, VMEM, VMEM, VMEM, VMEM),
        scratch_shapes=[
            pltpu.VMEM((8, 2, 64, 512), BF16),
            pltpu.VMEM((8, 2, 4, 64, 512), BF16),
            pltpu.VMEM((8, 2, 4, 64, 256), BF16),
            pltpu.VMEM((4, 128), F32),
            dma, dma((2,)), dma((8,)),
            dma((2, 4)), dma((2,)), dma((4,)), dma, dma((2, 7)), dma((2, 8)),
            dma, dma, dma((7,)), dma((8,)), dma, dma, dma((2,)), dma((2,)), dma((7,)), dma((8,)),
        ],
        compiler_params=pltpu.CompilerParams(
            collective_id=0, has_side_effects=True, vmem_limit_bytes=VMEM_LIMIT
        ),
        name="gather_factor",
    )(x, s)


def split(value):
    high = value.astype(BF16)
    return high, (value - high.astype(F32)).astype(BF16)


def dot(left, right):
    return jnp.dot(left, right, preferred_element_type=F32)


def schur_kernel(
    rows_ref, cols_ref, lead_ref, leadt_ref, w_ref, s_ref,
    out_ref, trace_ref,
    wide, tall, left, right,
):
    l = pl.program_id(0)
    r = lax.axis_index(ROW)
    c = lax.axis_index(COL)
    f = lax.axis_index("x_hi")

    @pl.when(l == 0)
    def _():
        high, low = split(w_ref[...])
        wide[:, :512], wide[:, 512:1024], wide[:, 1024:] = high, low, high
        tall[...] = wide[...].T
        trace_ref[...] = jnp.zeros_like(trace_ref)
        for m in range(4):
            points = cols_ref[:, :, m].reshape(1024, 256)
            high, low = split(dot(lead_ref[...], points))
            high, low = split(-dot(wide[...], jnp.concatenate([high, high, low], 0)))
            right[m, :1024] = points
            right[m, 1024:1536], right[m, 1536:2048], right[m, 2048:] = high, low, high

    points = rows_ref[...].reshape(1024, 512).T
    left[:, :1024] = points
    first = dot(points, leadt_ref[...])
    corner = (l == 0) & (r == 0)
    noise = s_ref[0]
    diag = lax.broadcasted_iota(jnp.int32, (512, 512), 0) == lax.broadcasted_iota(jnp.int32, (512, 512), 1)
    first = first + jnp.where(diag & corner, noise, 0.0)
    high, low = split(first)
    panel = dot(jnp.concatenate([high, high, low], 1), tall[...])
    high, low = split(panel)
    left[:, 1024:1536], left[:, 1536:2048], left[:, 2048:] = high, high, low

    @pl.when(jnp.logical_not(corner))
    def _():
        given = points.astype(F32)
        total = jnp.sum(given * given, axis=0, keepdims=True)
        minus = jnp.sum(panel * panel, axis=0, keepdims=True)
        trace_ref[...] += total[:, :512] + total[:, 512:] + noise - minus

    near = lax.broadcasted_iota(jnp.int32, (512, 256), 0) == lax.broadcasted_iota(jnp.int32, (512, 256), 1) + f * 256
    for m in range(4):
        def put(value):
            for half in range(2):
                out_ref[pl.ds(m * 2 + half, 512, stride=8), :] = value[:, half * 128 : half * 128 + 128]

        is_panel = (c == 0) & (m == 0)
        inside = (l > m) | ((l == m) & (r > c))
        same = (l == m) & (r == c)

        def value():
            return dot(left[...], right[m])

        @pl.when(is_panel)
        def _():
            for half in range(2):
                high = left[:, pl.ds(pl.multiple_of(1024 + f * 256 + half * 128, 128), 128)]
                low = left[:, pl.ds(pl.multiple_of(2048 + f * 256 + half * 128, 128), 128)]
                out_ref[pl.ds(m * 2 + half, 512, stride=8), :] = high.astype(F32) + low.astype(F32)

        @pl.when(inside & jnp.logical_not(is_panel))
        def _():
            put(value())

        @pl.when(same & jnp.logical_not(is_panel))
        def _():
            here = jnp.where(f == 0, noise[:, :256], noise[:, 256:])
            put(value() + jnp.where(near, here, 0.0))

        @pl.when(jnp.logical_not(inside | same))
        def _():
            put(jnp.zeros((512, 256), F32))


def schur(rows, cols, lead, leadt, w, s):
    return pl.pallas_call(
        schur_kernel,
        grid=(4,),
        out_shape=(
            jax.ShapeDtypeStruct((4 * 512 * 8, 128), F32),
            jax.ShapeDtypeStruct((1, 512), F32),
        ),
        in_specs=[
            pl.BlockSpec((8, 2, None, 64, 512), lambda l: (0, 0, l, 0, 0)),
            VMEM, VMEM, VMEM, VMEM,
            pl.BlockSpec((1, 1, 512), lambda l: (l, 0, 0)),
        ],
        out_specs=(
            pl.BlockSpec((512 * 8, 128), lambda l: (l, 0)),
            pl.BlockSpec((1, 512), lambda l: (0, 0)),
        ),
        scratch_shapes=[
            pltpu.VMEM((512, 1536), BF16),
            pltpu.VMEM((1536, 512), BF16),
            pltpu.VMEM((512, 2560), BF16),
            pltpu.VMEM((4, 2560, 256), BF16),
        ],
        compiler_params=pltpu.CompilerParams(vmem_limit_bytes=VMEM_LIMIT),
        name="schur",
    )(rows, cols, lead, leadt, w, s)


def total_kernel(trace_ref, log_ref, mean_ref, det_ref, slots, own_sem, send, recv):
    a, b = lax.axis_index("x_lo"), lax.axis_index("y")
    own = a * 4 + b

    def peer(d):
        return {"x_lo": (a + d // 4) % 2, "y": (b + d % 4) % 4}

    keep = pltpu.make_async_copy(trace_ref, slots.at[own], own_sem)
    keep.start()
    barrier = pltpu.get_barrier_semaphore()
    for d in range(1, 8):
        pl.semaphore_signal(barrier, inc=1, device_id=peer(d), device_id_type=IDS)
    pl.semaphore_wait(barrier, 7)
    pieces = [remote(trace_ref, slots.at[own], send.at[d - 1], recv.at[own], peer(d)) for d in range(1, 8)]
    for piece in pieces:
        piece.start()
    det_ref[0, 0] = jnp.sum(log_ref[:, 0:1])
    keep.wait()
    for d in range(1, 8):
        q = ((a + d // 4) % 2) * 4 + (b + d % 4) % 4
        pltpu.make_async_copy(slots.at[q], slots.at[q], recv.at[q]).wait()
    mean_ref[0, 0] = jnp.sum(slots[...]) / F32(32 * 512 - 512)
    for piece in pieces:
        piece.wait_send()


def totals(trace, logs):
    dma = pltpu.SemaphoreType.DMA
    scalar = jax.ShapeDtypeStruct((1, 1), F32)
    smem = pl.BlockSpec(memory_space=pltpu.SMEM)
    return pl.pallas_call(
        total_kernel,
        out_shape=(scalar, scalar),
        in_specs=[ANY, VMEM],
        out_specs=(smem, smem),
        scratch_shapes=[pltpu.VMEM((8, 1, 512), F32), dma, dma((7,)), dma((8,))],
        compiler_params=pltpu.CompilerParams(collective_id=1, has_side_effects=True),
        name="totals",
    )(trace, logs)


def shards(points, point_noise):
    x = jnp.swapaxes(points[:, 0], 1, 2)
    s = point_noise.reshape(4, 512)
    rows, cols, lead, leadt, w, logs = gather(x, s.reshape(4, 4, 128))
    out, trace = schur(rows, cols, lead, leadt, w, s.reshape(4, 1, 512))
    mean, det = totals(trace, logs)
    return out.reshape(4, 1, 512, 4, 1, 256), mean.reshape(()), det.reshape(())


def solution(mesh):
    torus = Mesh(mesh.devices.reshape(2, 4, 4, 2, mesh.shape["feat"]), AXES)
    return jax.shard_map(
        shards,
        mesh=torus,
        in_specs=(P(None, ROW, None, ("z", "core", "x_hi")), P(None, ROW, None)),
        out_specs=(P(None, ROW, None, None, COL, "x_hi"), P(), P()),
        check_vma=False,
    )
```

time: 121 us -> 98.8 us (0.82)
  the two profiles are of different devices: /device:TPU:38 before, /device:TPU:7 now
where the time goes in v2:
time: 98.8 us; the launch traced here: 97.3 us
  Pallas kernels  93.2 us (94%)
  between operations  4.14 us (4%)
    pallas_call x1, Pallas kernels, gather(): pl.pallas_call(gather_kernel, out_shape=(jax.ShapeDtypeStruct((8, 2, 4, 6...  60.9 us
    pallas_call x1, Pallas kernels, schur(): pl.pallas_call(schur_kernel, grid=(4,), out_shape=(jax.ShapeDtypeStruct((...  25.6 us
    pallas_call x1, Pallas kernels, totals(): pl.pallas_call(total_kernel, out_shape=(scalar, scalar), in_specs=[ANY, V...  6.73 us

profile of v2, /device:TPU:7, one launch (start us, length us, event | category | flops | bytes accessed | tf_op | source)
XLA Modules:
  0.0 97.3 jit_solution(13503092062762700155)
XLA Ops:
  0.6 60.9 %gather_factor.1 = (bf16[8,2,4,64,512]{4,3,2,1,0:T(8,128)(2,1)}, bf16[8,2,4,64,256]{4,3,2,1,0:T(8,128)(2,1)}, bf16[512,1024]{1,0:T(8,128)(2,1)}, bf16[1024,512]{...) custom-call(bf16[4,64,512]{2,1,0:T(8,128)(2,1)} %bitcast.7, f32[4,4,128]{2,1,0:T(4,128)} %bitcast.8), custom_call_target="tpu_custom_call" | custom-call | tf_op jit(solution)/shard_map/gather_factor/pallas_call | solution.py:369
  61.5 25.6 %schur.1 = (f32[16384,128]{1,0:T(8,128)}, f32[1,512]{1,0:T(1,128)}) custom-call(bf16[8,2,4,64,512]{4,3,2,1,0:T(8,128)(2,1)} %get-tuple-element.13.rows_ref, bf16[8,2,4,64,256]{4,3,2,1,0:T(8,128)(2,1)} %get-tuple-element.14.cols_ref, bf16[512,1024]{1,0:T(8,128)(2,1)} %get-tuple-element.15.lead_ref, bf16[1024,512]{1,0:T(8,128)(2,1)} %get-tuple-element.16.leadt_ref, ...), custom_call_target="tpu_custom_call" | custom-call | tf_op jit(solution)/shard_map/schur/pallas_call | solution.py:483
  87.1 6.7 %totals.1 = (f32[1,1]{1,0:T(1,128)}, f32[1,1]{1,0:T(1,128)}) custom-call(f32[1,512]{1,0:T(1,128)} %get-tuple-element.19.trace_ref, f32[8,128]{1,0:T(8,128)} %get-tuple-element.20.log_ref), custom_call_target="tpu_custom_call" | custom-call | tf_op jit(solution)/shard_map/totals/pallas_call | solution.py:540

commit v3 on v2

v3 whole, which is shorter than its diff:
```python
import jax
import jax.numpy as jnp
from jax import lax
from jax.experimental import pallas as pl
from jax.experimental.pallas import tpu as pltpu
from jax.sharding import Mesh
from jax.sharding import PartitionSpec as P

F32 = jnp.float32
BF16 = jnp.bfloat16
HIGHEST = lax.Precision.HIGHEST
IDS = pl.DeviceIdType.MESH
AXES = ("x_lo", "y", "z", "core", "x_hi")
ROW = ("x_lo", "y")
COL = ("z", "core")
VMEM = pl.BlockSpec(memory_space=pltpu.VMEM)
ANY = pl.BlockSpec(memory_space=pl.ANY)
VMEM_LIMIT = 60 * 1024 * 1024


def factor_block(block, hook):
    lane = lax.broadcasted_iota(jnp.int32, (8, 128), 1)
    sub = lax.broadcasted_iota(jnp.int32, (8, 128), 0)
    rows, logs = [], jnp.zeros((8, 128), F32)
    top, below = block[:8], block[8:]
    for k in range(16):
        c, n = 8 * k, 120 - 8 * k
        if k == 8:
            hook()
        diag = [jnp.broadcast_to(top[:, c + t : c + t + 1], (8, 128)) for t in range(8)]
        here = (lane >= c) & (lane < c + 8)
        top = jnp.where(here, jnp.where(lane - c == sub, 1.0, 0.0), top)
        if n:
            cols = [jnp.broadcast_to(below[:, c + t : c + t + 1], (n, 128)) for t in range(8)]
            wide = lax.broadcasted_iota(jnp.int32, (n, 128), 1)
            below = jnp.where((wide >= c) & (wide < c + 8), 0.0, below)
        pivots = jnp.zeros((8, 128), F32)
        for t in range(8):
            pivot = diag[t][t : t + 1, :]
            inv = 1.0 / pivot
            pivots = jnp.where(sub == t, pivot, pivots)
            factor = jnp.where(sub > t, diag[t] * inv, 0.0)
            row = top[t : t + 1, :]
            ends = [diag[j][t : t + 1, :] for j in range(8)]
            for j in range(t + 1, 8):
                diag[j] = diag[j] - factor * ends[j]
            top = top - factor * row
            if n:
                scaled = cols[t] * inv
                below = below - scaled * row
                for j in range(t + 1, 8):
                    cols[j] = cols[j] - scaled * ends[j]
        rows.append(jnp.where(lane < c + 8, top, 0.0) * lax.rsqrt(pivots))
        logs = logs + jnp.log(pivots)
        if n:
            top, below = below[:8], below[8:]
    return jnp.concatenate(rows, 0), logs


def factor_step(k, w_ref, log_ref, hook, between):
    n = w_ref.shape[0]
    at = pl.ds(pl.multiple_of(k * 128, 128), 128)
    block, logs = factor_block(w_ref[at, at], hook)
    log_ref[...] += logs
    between()
    col_block = lax.broadcasted_iota(jnp.int32, (128, n), 1) // 128
    lead = jnp.dot(block, w_ref[at, :], precision=HIGHEST)
    lead = jnp.where(col_block == k, jnp.concatenate([block] * (n // 128), 1), lead)

    @pl.when(k < n // 128 - 1)
    def _():
        row_block = lax.broadcasted_iota(jnp.int32, (n, 128), 0) // 128
        all_block = lax.broadcasted_iota(jnp.int32, (n, n), 1) // 128
        left = lax.dot_general(w_ref[:, at], block, (((1,), (1,)), ((), ())), precision=HIGHEST)
        left = jnp.where(row_block > k, left, 0.0)
        rest = jnp.where(all_block == k, 0.0, w_ref[...])
        w_ref[...] = rest - jnp.dot(left, lead, precision=HIGHEST)

    w_ref[at, :] = lead


def split(value):
    high = value.astype(BF16)
    return high, (value - high.astype(F32)).astype(BF16)


def dot(left, right):
    return jnp.dot(left, right, preferred_element_type=F32)


def remote(src, dst, send, recv, to):
    return pltpu.make_async_remote_copy(
        src_ref=src, dst_ref=dst, send_sem=send, recv_sem=recv, device_id=to, device_id_type=IDS
    )


def gather_kernel(
    x_ref, s_ref,
    points_out, cols_out, panel_out, cross_out, mean_ref, det_ref,
    lead, rows, cols, noise, own_noise, lead_out, w_ref, log_ref, wide, tall, points, panel, cross, slots,
    own_sem, noise_sem, row_out, col_out, trace_send, trace_recv, share_send, share_recv, lead_send, lead_recv, noise_send, noise_recv, line_send, line_recv,
    swap_send, swap_recv, row_send, row_recv, rswap_send, rswap_recv, spread_send, spread_recv, col_send, col_recv,
):
    a, b, z, k, h = (lax.axis_index(name) for name in AXES)
    q_line = z * 2 + h
    partner = {"core": 1 - k}

    def plane(d):
        return {"x_lo": (a + d // 4) % 2, "y": (b + d % 4) % 4}

    def line(d):
        return {"x_hi": (h + d // 4) % 2, "z": (z + d % 4) % 4}

    row_group = a * 4 + b
    to_z, to_k = row_group // 2, row_group % 2
    to_a, to_b = (a + h) % 2, (b + z) % 4
    col_group = z * 2 + k
    from_a, from_b = col_group // 4, col_group % 4

    def spread_to(f):
        return {"x_lo": to_a, "y": to_b, "z": to_z, "core": to_k, "x_hi": f}

    def spread_self(f):
        return (a == to_a) & (b == to_b) & (z == to_z) & (k == to_k) & (h == f)

    def spread_from(kk):
        return {"x_lo": from_a, "y": from_b, "z": (b + 4 - from_b) % 4, "core": kk, "x_hi": (a + from_a) % 2}

    def from_self(kk):
        return (
            (a == from_a) & (b == from_b) & (z == (b + 4 - from_b) % 4) & (k == kk) & (h == (a + from_a) % 2)
        )

    def q_at(da, db):
        return ((b + db + 4 - from_b) % 4) * 2 + (a + da + from_a) % 2

    def q_on(j, db):
        return ((b + db + 4 - from_b) % 4) * 2 + (j + from_a) % 2

    q_plane = q_at(0, 0)

    own_row = pltpu.make_async_copy(x_ref, rows.at[q_line, k], own_sem)
    own_row.start()
    own_s = pltpu.make_async_copy(s_ref, own_noise, noise_sem)
    own_s.start()

    barrier = pltpu.get_barrier_semaphore()
    for d in range(1, 8):
        pl.semaphore_signal(barrier, inc=1, device_id=plane(d), device_id_type=IDS)
        pl.semaphore_signal(barrier, inc=1, device_id=line(d), device_id_type=IDS)
        pl.semaphore_signal(barrier, inc=1, device_id=plane(d) | partner, device_id_type=IDS)
    pl.semaphore_signal(barrier, inc=1, device_id=partner, device_id_type=IDS)
    for i in range(2):
        @pl.when(jnp.logical_not(spread_self(i)))
        def _():
            pl.semaphore_signal(barrier, inc=1, device_id=spread_to(i), device_id_type=IDS)

        @pl.when(jnp.logical_not(from_self(i)))
        def _():
            pl.semaphore_signal(barrier, inc=1, device_id=spread_from(i), device_id_type=IDS)

    selfish = spread_self(0) | spread_self(1)

    @pl.when(selfish)
    def _():
        pl.semaphore_wait(barrier, 24)

    @pl.when(jnp.logical_not(selfish))
    def _():
        pl.semaphore_wait(barrier, 26)

    def row_piece(q, slot, to):
        src = x_ref if slot < 4 else rows.at[q, k]
        return remote(src, rows.at[q, k], row_send.at[slot], row_recv.at[q], to)

    def row_wait(q):
        pltpu.make_async_copy(rows.at[q, k], rows.at[q, k], row_recv.at[q]).wait()

    def col_piece(q, slot, to):
        return remote(cols.at[q], cols.at[q], col_send.at[slot], col_recv.at[q], to)

    def col_wait(q):
        pltpu.make_async_copy(cols.at[q], cols.at[q], col_recv.at[q]).wait()

    put_cols = pltpu.make_async_copy(cols, cols_out, col_out)

    def put_points(l):
        return pltpu.make_async_copy(points.at[l], points_out.at[l], row_out.at[0, l])

    def put_panel(l):
        return pltpu.make_async_copy(panel.at[l], panel_out.at[l], row_out.at[1, l])

    def put_cross(m):
        return pltpu.make_async_copy(cross.at[m], cross_out.at[m], row_out.at[2, m])

    own_slot = row_group * 2 + k

    def trace_piece(d):
        own = slots.at[own_slot]
        to = plane(d % 8) | {"core": (k + d // 8) % 2}
        return remote(own, own, trace_send.at[d - 1], trace_recv.at[own_slot], to)

    def share_piece(j):
        l = k * 2 + j
        return remote(panel.at[l], panel.at[l], share_send.at[j], share_recv.at[l], partner)

    def over_z(d):
        return {"z": (z + d) % 4}

    def over_y(d):
        return {"y": (b + d) % 4}

    q_pair = z * 2 + 1 - h
    q_cross = q_at(1, 0)

    root = b == 0
    source = root & (a == 0)

    def lead_part(q, i):
        return lead.at[q, k, :, pl.ds(128 * i, 128 + 256 * i)]

    def lead_piece(i, d, to):
        dst = lead_part(q_line, i)
        return remote(dst, dst, lead_send.at[i, d], lead_recv.at[i], to)

    def noise_piece(d, to):
        return remote(noise, noise, noise_send.at[d], noise_recv, to)

    @pl.when(source)
    def _():
        for i in range(2):
            given = x_ref.at[0, :, pl.ds(128 * i, 128 + 256 * i)]
            pltpu.make_async_copy(given, lead_part(q_line, i), lead_recv.at[i]).start()
        pltpu.make_async_copy(s_ref.at[0], noise, noise_recv).start()

    def lead_wait(i):
        part = lead_part(q_line, i)
        pltpu.make_async_copy(part, part, lead_recv.at[i]).wait()
        if i == 1:
            pltpu.make_async_copy(noise, noise, noise_recv).wait()

        @pl.when(source)
        def _():
            lead_piece(i, 0, {"x_lo": 1 - a}).start()
            if i == 1:
                noise_piece(0, {"x_lo": 1 - a}).start()

        @pl.when(root)
        def _():
            for d in range(1, 4):
                lead_piece(i, d, {"y": (b + d) % 4}).start()
            if i == 1:
                for d in range(1, 4):
                    noise_piece(d, {"y": (b + d) % 4}).start()

    def spread():
        for f in range(2):
            half = x_ref.at[:, :, f * 256 : f * 256 + 256]
            place = cols.at[q_line, k]

            @pl.when(spread_self(f))
            def _():
                pltpu.make_async_copy(half, place, spread_recv.at[k]).start()

            @pl.when(jnp.logical_not(spread_self(f)))
            def _():
                remote(half, place, spread_send.at[f], spread_recv.at[k], spread_to(f)).start()

    pl.when(jnp.logical_not(root))(spread)
    for d in (1, 3):
        row_piece(q_line, d, over_z(d)).start()

    def line_piece(i, d):
        part = lead_part(q_line, i)
        return remote(part, part, line_send.at[i, d - 1], line_recv.at[i, q_line], line(d))

    for i in range(2):
        lead_wait(i)
        for d in range(1, 8):
            line_piece(i, d).start()
    pl.when(root)(spread)

    def line_wait(i):
        for d in range(1, 8):
            q = ((z + d % 4) % 4) * 2 + (h + d // 4) % 2
            pltpu.make_async_copy(lead_part(q, i), lead_part(q, i), line_recv.at[i, q]).wait()

    def swap_piece(i):
        part = lead.at[:, k, :, pl.ds(128 * i, 128 + 256 * i)]
        return remote(part, part, swap_send.at[i], swap_recv.at[i], partner)

    def swap_wait(i):
        part = lead.at[:, k, :, pl.ds(128 * i, 128 + 256 * i)]
        pltpu.make_async_copy(part, part, swap_recv.at[i]).wait()

    diag = lax.broadcasted_iota(jnp.int32, (128, 128), 0) == lax.broadcasted_iota(jnp.int32, (128, 128), 1)
    log_ref[...] = jnp.zeros_like(log_ref)
    line_wait(0)
    swap_piece(0).start()
    for kk in range(2):
        pltpu.make_async_copy(cols.at[q_plane, kk], cols.at[q_plane, kk], spread_recv.at[kk]).wait()
    col_piece(q_plane, 0, {"x_lo": 1 - a}).start()
    for d in (1, 3, 2):
        col_piece(q_plane, d, over_y(d)).start()
    swap_wait(0)
    some = lead[:, :, :, :128].reshape(1024, 128)
    lead_out[:128, :] = some.T
    w_ref[:128, :128] = dot(lead_out[:128, :], some) + jnp.where(diag, noise[0:1, :], 0.0)

    def middle_first():
        line_wait(1)
        swap_piece(1).start()
        row_piece(q_line, 0, {"x_hi": 1 - h}).start()
        row_piece(q_line, 2, over_z(2)).start()

    def after_first():
        col_wait(q_cross)
        for d in (1, 3, 2):
            col_piece(q_cross, 3 + d, over_y(d)).start()
        own_row.wait()
        own_s.wait()
        swap_wait(1)
        some = lead[:, :, :, 128:].reshape(1024, 384)
        lead_out[128:, :] = some.T
        w_ref[:128, 128:] = dot(lead_out[:128, :], some)
        for i in range(1, 4):
            block = slice(i * 128, i * 128 + 128)
            w_ref[block, :] = dot(lead_out[block, :], lead[...].reshape(1024, 512))
            w_ref[block, block] += jnp.where(diag, noise[i : i + 1, :], 0.0)

    def middle_second():
        row_wait(q_pair)
        for d in (2, 1, 3):
            row_piece(q_pair, 3 + d, over_z(d)).start()

    def middle_last():
        for d in range(1, 4):
            for j in range(2):
                col_wait(q_on(j, d))
        put_cols.start()
        for d in range(1, 4):
            for j in range(2):
                row_wait(((z + d) % 4) * 2 + j)
        remote(rows.at[:, k], rows.at[:, k], rswap_send, rswap_recv, partner).start()

    def step(i, carry):
        def hook():
            pl.when(i == 0)(middle_first)
            pl.when(i == 1)(middle_second)
            pl.when(i == 3)(middle_last)

        factor_step(i, w_ref, log_ref, hook, lambda: pl.when(i == 0)(after_first))
        return carry

    lax.fori_loop(0, 4, step, 0)
    n = w_ref.shape[0]
    lower = lax.broadcasted_iota(jnp.int32, (n, n), 0) >= lax.broadcasted_iota(jnp.int32, (n, n), 1)
    high, low = split(jnp.where(lower, w_ref[...], 0.0))
    wide[:, :512], wide[:, 512:1024], wide[:, 1024:] = high, low, high
    tall[...] = wide[...].T
    det_ref[0, 0] = jnp.sum(log_ref[:, 0:1])
    slots[own_slot] = jnp.zeros((1, 512), F32)

    pltpu.make_async_copy(rows.at[:, k], rows.at[:, k], rswap_recv).wait()

    def row_step(j, carry):
        l = k * 2 + j
        given = rows[:, :, l].reshape(1024, 512).T
        points[l] = given
        first = dot(given, lead[...].reshape(1024, 512))
        corner = (l == 0) & (row_group == 0)
        eye = lax.broadcasted_iota(jnp.int32, (512, 512), 0) == lax.broadcasted_iota(jnp.int32, (512, 512), 1)
        s = jnp.concatenate([own_noise[l, i : i + 1] for i in range(4)], 1)
        first = first + jnp.where(eye & corner, s, 0.0)
        high, low = split(first)
        value = dot(jnp.concatenate([high, high, low], 1), tall[...])
        high, low = split(value)
        panel[l, :, :512], panel[l, :, 512:] = high, low

        @pl.when(jnp.logical_not(corner))
        def _():
            wider = given.astype(F32)
            total = jnp.sum(wider * wider, axis=0, keepdims=True)
            minus = jnp.sum(value * value, axis=0, keepdims=True)
            slots[own_slot] += total[:, :512] + total[:, 512:] + s - minus

        put_points(l).start()
        put_panel(l).start()
        return carry

    lax.fori_loop(0, 2, row_step, 0)

    def other_step(j, carry):
        l = (1 - k) * 2 + j
        points[l] = rows[:, :, l].reshape(1024, 512).T
        put_points(l).start()
        return carry

    share_piece(0).start()
    lax.fori_loop(0, 2, other_step, 0)
    share_piece(1).start()

    def col_step(m):
        high, low = split(dot(lead_out[...], cols[:, :, m].reshape(1024, 256)))
        high, low = split(-dot(wide[...], jnp.concatenate([high, high, low], 0)))
        cross[m, :512], cross[m, 512:] = high, low
        put_cross(m).start()

    col_step(0)
    for d in range(1, 16):
        trace_piece(d).start()
    col_step(1)
    for j in range(2):
        l = (1 - k) * 2 + j
        pltpu.make_async_copy(panel.at[l], panel.at[l], share_recv.at[l]).wait()
        put_panel(l).start()
    col_step(2)
    col_step(3)
    for d in range(1, 16):
        q = (((a + d % 8 // 4) % 2) * 4 + (b + d % 4) % 4) * 2 + (k + d // 8) % 2
        pltpu.make_async_copy(slots.at[q], slots.at[q], trace_recv.at[q]).wait()
    mean_ref[0, 0] = jnp.sum(slots[...]) / F32(32 * 512 - 512)

    for i in range(2):
        @pl.when(source)
        def _():
            lead_piece(i, 0, partner).wait_send()

        @pl.when(root)
        def _():
            for d in range(1, 4):
                lead_piece(i, d, partner).wait_send()

        for d in range(1, 8):
            line_piece(i, d).wait_send()

    @pl.when(source)
    def _():
        noise_piece(0, partner).wait_send()

    @pl.when(root)
    def _():
        for d in range(1, 4):
            noise_piece(d, partner).wait_send()

    for i in range(2):
        swap_piece(i).wait_send()
        share_piece(i).wait_send()
    for i in range(7):
        row_piece(q_line, i, partner).wait_send()
        col_piece(q_plane, i, partner).wait_send()
    for d in range(1, 16):
        trace_piece(d).wait_send()
    for f in range(2):
        @pl.when(jnp.logical_not(spread_self(f)))
        def _():
            half = x_ref.at[:, :, f * 256 : f * 256 + 256]
            remote(half, cols.at[q_line, k], spread_send.at[f], spread_recv.at[k], spread_to(f)).wait_send()

    remote(rows.at[:, k], rows.at[:, k], rswap_send, rswap_recv, partner).wait_send()
    put_cols.wait()
    for j in range(4):
        put_points(j).wait()
        put_panel(j).wait()
        put_cross(j).wait()


def gather(x, s):
    dma = pltpu.SemaphoreType.DMA
    scalar = jax.ShapeDtypeStruct((1, 1), F32)
    smem = pl.BlockSpec(memory_space=pltpu.SMEM)
    return pl.pallas_call(
        gather_kernel,
        out_shape=(
            jax.ShapeDtypeStruct((4, 512, 1024), BF16),
            jax.ShapeDtypeStruct((8, 2, 4, 64, 256), BF16),
            jax.ShapeDtypeStruct((4, 512, 1024), BF16),
            jax.ShapeDtypeStruct((4, 1024, 256), BF16),
            scalar,
            scalar,
        ),
        in_specs=[ANY, ANY],
        out_specs=(ANY, ANY, ANY, ANY, smem, smem),
        scratch_shapes=[
            pltpu.VMEM((8, 2, 64, 512), BF16),
            pltpu.VMEM((8, 2, 4, 64, 512), BF16),
            pltpu.VMEM((8, 2, 4, 64, 256), BF16),
            pltpu.VMEM((4, 128), F32),
            pltpu.VMEM((4, 4, 128), F32),
            pltpu.VMEM((512, 1024), BF16),
            pltpu.VMEM((512, 512), F32),
            pltpu.VMEM((8, 128), F32),
            pltpu.VMEM((512, 1536), BF16),
            pltpu.VMEM((1536, 512), BF16),
            pltpu.VMEM((4, 512, 1024), BF16),
            pltpu.VMEM((4, 512, 1024), BF16),
            pltpu.VMEM((4, 1024, 256), BF16),
            pltpu.VMEM((16, 1, 512), F32),
            dma, dma, dma((3, 4)), dma, dma((15,)), dma((16,)), dma((2,)), dma((4,)),
            dma((2, 4)), dma((2,)), dma((4,)), dma, dma((2, 7)), dma((2, 8)),
            dma((2,)), dma((2,)), dma((7,)), dma((8,)), dma, dma, dma((2,)), dma((2,)), dma((7,)), dma((8,)),
        ],
        compiler_params=pltpu.CompilerParams(
            collective_id=0, has_side_effects=True, vmem_limit_bytes=VMEM_LIMIT
        ),
        name="gather_factor",
    )(x, s)


def schur_kernel(points_ref, cols_ref, panel_ref, cross_ref, s_ref, out_ref):
    l = pl.program_id(0)
    r = lax.axis_index(ROW)
    c = lax.axis_index(COL)
    f = lax.axis_index("x_hi")
    noise = s_ref[0]
    near = lax.broadcasted_iota(jnp.int32, (512, 256), 0) == lax.broadcasted_iota(jnp.int32, (512, 256), 1) + f * 256
    for m in range(4):
        def put(value):
            for half in range(2):
                out_ref[pl.ds(m * 2 + half, 512, stride=8), :] = value[:, half * 128 : half * 128 + 128]

        is_panel = (c == 0) & (m == 0)
        inside = (l > m) | ((l == m) & (r > c))
        same = (l == m) & (r == c)

        def value():
            high = cross_ref[m, :512]
            total = dot(points_ref[...], cols_ref[:, :, m].reshape(1024, 256))
            total = total + dot(panel_ref[...], jnp.concatenate([high, high], 0))
            return total + dot(panel_ref[:, :512], cross_ref[m, 512:])

        @pl.when(is_panel)
        def _():
            for half in range(2):
                high = panel_ref[:, pl.ds(pl.multiple_of(f * 256 + half * 128, 128), 128)]
                low = panel_ref[:, pl.ds(pl.multiple_of(512 + f * 256 + half * 128, 128), 128)]
                out_ref[pl.ds(m * 2 + half, 512, stride=8), :] = high.astype(F32) + low.astype(F32)

        @pl.when(inside & jnp.logical_not(is_panel))
        def _():
            put(value())

        @pl.when(same & jnp.logical_not(is_panel))
        def _():
            here = jnp.where(f == 0, noise[:, :256], noise[:, 256:])
            put(value() + jnp.where(near, here, 0.0))

        @pl.when(jnp.logical_not(inside | same))
        def _():
            put(jnp.zeros((512, 256), F32))


def schur(points, cols, panel, cross, s):
    tile = pl.BlockSpec((None, 512, 1024), lambda l: (l, 0, 0))
    return pl.pallas_call(
        schur_kernel,
        grid=(4,),
        out_shape=jax.ShapeDtypeStruct((4 * 512 * 8, 128), F32),
        in_specs=[tile, VMEM, tile, VMEM, pl.BlockSpec((1, 1, 512), lambda l: (l, 0, 0))],
        out_specs=pl.BlockSpec((512 * 8, 128), lambda l: (l, 0)),
        compiler_params=pltpu.CompilerParams(vmem_limit_bytes=VMEM_LIMIT),
        name="schur",
    )(points, cols, panel, cross, s)


def shards(points, point_noise):
    x = jnp.swapaxes(points[:, 0], 1, 2)
    s = point_noise.reshape(4, 512)
    given, cols, panel, cross, mean, det = gather(x, s.reshape(4, 4, 128))
    out = schur(given, cols, panel, cross, s.reshape(4, 1, 512))
    return out.reshape(4, 1, 512, 4, 1, 256), mean.reshape(()), det.reshape(())


def solution(mesh):
    torus = Mesh(mesh.devices.reshape(2, 4, 4, 2, mesh.shape["feat"]), AXES)
    return jax.shard_map(
        shards,
        mesh=torus,
        in_specs=(P(None, ROW, None, ("z", "core", "x_hi")), P(None, ROW, None)),
        out_specs=(P(None, ROW, None, None, COL, "x_hi"), P(), P()),
        check_vma=False,
    )
```

time: 98.8 us -> 86.1 us (0.87)
  the two profiles are of different devices: /device:TPU:7 before, /device:TPU:9 now
where the time goes in v3:
time: 86.1 us; the launch traced here: 85.9 us
  Pallas kernels  81.7 us (95%)
  between operations  4.19 us (5%)
    pallas_call x1, Pallas kernels, gather(): pl.pallas_call(gather_kernel, out_shape=(jax.ShapeDtypeStruct((4, 512, 10...  67.1 us
    pallas_call x1, Pallas kernels, schur(): pl.pallas_call(schur_kernel, grid=(4,), out_shape=jax.ShapeDtypeStruct((4...  14.6 us

profile of v3, /device:TPU:9, one launch (start us, length us, event | category | flops | bytes accessed | tf_op | source)
XLA Modules:
  0.0 85.9 jit_solution(17424228364958052022)
XLA Ops:
  0.6 67.1 %gather_factor.1 = (bf16[4,512,1024]{2,1,0:T(8,128)(2,1)}, bf16[8,2,4,64,256]{4,3,2,1,0:T(8,128)(2,1)}, bf16[4,512,1024]{2,1,0:T(8,128)(2,1)}, bf16[4,1024,256]{...) custom-call(bf16[4,64,512]{2,1,0:T(8,128)(2,1)} %bitcast.8, f32[4,4,128]{2,1,0:T(4,128)} %bitcast.9), custom_call_target="tpu_custom_call" | custom-call | tf_op jit(solution)/shard_map/gather_factor/pallas_call | solution.py:472
  67.7 14.6 %schur.1 = f32[16384,128]{1,0:T(8,128)} custom-call(bf16[4,512,1024]{2,1,0:T(8,128)(2,1)} %get-tuple-element.9.points_ref, bf16[8,2,4,64,256]{4,3,2,1,0:T(8,128)(2,1)} %get-tuple-element.10.cols_ref, bf16[4,512,1024]{2,1,0:T(8,128)(2,1)} %get-tuple-element.11.panel_ref, bf16[4,1024,256]{2,1,0:T(8,128)(2,1)} %get-tuple-element.12.cross_ref, f32[4,1,512]{2,1,0:T(1,128)} %s_ref.1), custom_call_target="tpu_custom_call" | custom-call | tf_op jit(solution)/shard_map/schur/pallas_call | solution.py:555

commit v4 on v3

--- a/solution.py
+++ b/solution.py
@@ -267,8 +267,6 @@
                 remote(half, place, spread_send.at[f], spread_recv.at[k], spread_to(f)).start()
 
     pl.when(jnp.logical_not(root))(spread)
-    for d in (1, 3):
-        row_piece(q_line, d, over_z(d)).start()
 
     def line_piece(i, d):
         part = lead_part(q_line, i)
@@ -297,6 +295,8 @@
     log_ref[...] = jnp.zeros_like(log_ref)
     line_wait(0)
     swap_piece(0).start()
+    for d in (1, 3):
+        row_piece(q_line, d, over_z(d)).start()
     for kk in range(2):
         pltpu.make_async_copy(cols.at[q_plane, kk], cols.at[q_plane, kk], spread_recv.at[kk]).wait()
     col_piece(q_plane, 0, {"x_lo": 1 - a}).start()

time: 86.1 us -> 84.3 us (0.979)
  the two profiles are of different devices: /device:TPU:9 before, /device:TPU:7 now
where the time goes in v4:
time: 84.3 us; the launch traced here: 83.9 us
  Pallas kernels  79.7 us (95%)
  between operations  4.19 us (5%)
    pallas_call x1, Pallas kernels, gather(): pl.pallas_call(gather_kernel, out_shape=(jax.ShapeDtypeStruct((4, 512, 10...  65.1 us
    pallas_call x1, Pallas kernels, schur(): pl.pallas_call(schur_kernel, grid=(4,), out_shape=jax.ShapeDtypeStruct((4...  14.6 us

profile of v4, /device:TPU:7, one launch (start us, length us, event | category | flops | bytes accessed | tf_op | source)
XLA Modules:
  0.0 83.9 jit_solution(17628425435978895067)
XLA Ops:
  0.6 65.1 %gather_factor.1 = (bf16[4,512,1024]{2,1,0:T(8,128)(2,1)}, bf16[8,2,4,64,256]{4,3,2,1,0:T(8,128)(2,1)}, bf16[4,512,1024]{2,1,0:T(8,128)(2,1)}, bf16[4,1024,256]{...) custom-call(bf16[4,64,512]{2,1,0:T(8,128)(2,1)} %bitcast.8, f32[4,4,128]{2,1,0:T(4,128)} %bitcast.9), custom_call_target="tpu_custom_call" | custom-call | tf_op jit(solution)/shard_map/gather_factor/pallas_call | solution.py:472
  65.8 14.6 %schur.1 = f32[16384,128]{1,0:T(8,128)} custom-call(bf16[4,512,1024]{2,1,0:T(8,128)(2,1)} %get-tuple-element.9.points_ref, bf16[8,2,4,64,256]{4,3,2,1,0:T(8,128)(2,1)} %get-tuple-element.10.cols_ref, bf16[4,512,1024]{2,1,0:T(8,128)(2,1)} %get-tuple-element.11.panel_ref, bf16[4,1024,256]{2,1,0:T(8,128)(2,1)} %get-tuple-element.12.cross_ref, f32[4,1,512]{2,1,0:T(1,128)} %s_ref.1), custom_call_target="tpu_custom_call" | custom-call | tf_op jit(solution)/shard_map/schur/pallas_call | solution.py:555

commit v5 on v4

--- a/solution.py
+++ b/solution.py
@@ -300,7 +300,7 @@
     for kk in range(2):
         pltpu.make_async_copy(cols.at[q_plane, kk], cols.at[q_plane, kk], spread_recv.at[kk]).wait()
     col_piece(q_plane, 0, {"x_lo": 1 - a}).start()
-    for d in (1, 3, 2):
+    for d in (1, 3):
         col_piece(q_plane, d, over_y(d)).start()
     swap_wait(0)
     some = lead[:, :, :, :128].reshape(1024, 128)
@@ -315,6 +315,7 @@
 
     def after_first():
         col_wait(q_cross)
+        col_piece(q_plane, 2, over_y(2)).start()
         for d in (1, 3, 2):
             col_piece(q_cross, 3 + d, over_y(d)).start()
         own_row.wait()
@@ -341,7 +342,16 @@
         for d in range(1, 4):
             for j in range(2):
                 row_wait(((z + d) % 4) * 2 + j)
-        remote(rows.at[:, k], rows.at[:, k], rswap_send, rswap_recv, partner).start()
+        for i in range(2):
+            row_swap(i).start()
+
+    def row_swap(i):
+        part = rows.at[:, k, pl.ds(2 * ((1 - k + i) % 2), 2)]
+        return remote(part, part, rswap_send.at[i], rswap_recv.at[i], partner)
+
+    def row_swap_wait(i):
+        part = rows.at[:, k, pl.ds(2 * ((k + i) % 2), 2)]
+        pltpu.make_async_copy(part, part, rswap_recv.at[i]).wait()
 
     def step(i, carry):
         def hook():
@@ -361,7 +371,7 @@
     det_ref[0, 0] = jnp.sum(log_ref[:, 0:1])
     slots[own_slot] = jnp.zeros((1, 512), F32)
 
-    pltpu.make_async_copy(rows.at[:, k], rows.at[:, k], rswap_recv).wait()
+    row_swap_wait(0)
 
     def row_step(j, carry):
         l = k * 2 + j
@@ -397,6 +407,7 @@
         return carry
 
     share_piece(0).start()
+    row_swap_wait(1)
     lax.fori_loop(0, 2, other_step, 0)
     share_piece(1).start()
 
@@ -457,7 +468,8 @@
             half = x_ref.at[:, :, f * 256 : f * 256 + 256]
             remote(half, cols.at[q_line, k], spread_send.at[f], spread_recv.at[k], spread_to(f)).wait_send()
 
-    remote(rows.at[:, k], rows.at[:, k], rswap_send, rswap_recv, partner).wait_send()
+    for i in range(2):
+        row_swap(i).wait_send()
     put_cols.wait()
     for j in range(4):
         put_points(j).wait()
@@ -498,7 +510,7 @@
             pltpu.VMEM((16, 1, 512), F32),
             dma, dma, dma((3, 4)), dma, dma((15,)), dma((16,)), dma((2,)), dma((4,)),
             dma((2, 4)), dma((2,)), dma((4,)), dma, dma((2, 7)), dma((2, 8)),
-            dma((2,)), dma((2,)), dma((7,)), dma((8,)), dma, dma, dma((2,)), dma((2,)), dma((7,)), dma((8,)),
+            dma((2,)), dma((2,)), dma((7,)), dma((8,)), dma((2,)), dma((2,)), dma((2,)), dma((2,)), dma((7,)), dma((8,)),
         ],
         compiler_params=pltpu.CompilerParams(
             collective_id=0, has_side_effects=True, vmem_limit_bytes=VMEM_LIMIT

time: 84.3 us -> 83 us (0.985)
  Pallas kernels: 79.7 us -> 78.6 us
    pallas_call x1, Pallas kernels: 65.1 us -> 64 us  [gather(): pl.pallas_call(gather_kernel, out_shape=(jax.ShapeDtypeStruct((4, 512, 10...]
where the time goes in v5:
time: 83 us; the launch traced here: 82.8 us
  Pallas kernels  78.6 us (95%)
  between operations  4.19 us (5%)
    pallas_call x1, Pallas kernels, gather(): pl.pallas_call(gather_kernel, out_shape=(jax.ShapeDtypeStruct((4, 512, 10...  64 us
    pallas_call x1, Pallas kernels, schur(): pl.pallas_call(schur_kernel, grid=(4,), out_shape=jax.ShapeDtypeStruct((4...  14.6 us

profile of v5, /device:TPU:7, one launch (start us, length us, event | category | flops | bytes accessed | tf_op | source)
XLA Modules:
  0.0 82.8 jit_solution(710160225573736502)
XLA Ops:
  0.6 64.0 %gather_factor.1 = (bf16[4,512,1024]{2,1,0:T(8,128)(2,1)}, bf16[8,2,4,64,256]{4,3,2,1,0:T(8,128)(2,1)}, bf16[4,512,1024]{2,1,0:T(8,128)(2,1)}, bf16[4,1024,256]{...) custom-call(bf16[4,64,512]{2,1,0:T(8,128)(2,1)} %bitcast.8, f32[4,4,128]{2,1,0:T(4,128)} %bitcast.9), custom_call_target="tpu_custom_call" | custom-call | tf_op jit(solution)/shard_map/gather_factor/pallas_call | solution.py:484
  64.6 14.6 %schur.1 = f32[16384,128]{1,0:T(8,128)} custom-call(bf16[4,512,1024]{2,1,0:T(8,128)(2,1)} %get-tuple-element.9.points_ref, bf16[8,2,4,64,256]{4,3,2,1,0:T(8,128)(2,1)} %get-tuple-element.10.cols_ref, bf16[4,512,1024]{2,1,0:T(8,128)(2,1)} %get-tuple-element.11.panel_ref, bf16[4,1024,256]{2,1,0:T(8,128)(2,1)} %get-tuple-element.12.cross_ref, f32[4,1,512]{2,1,0:T(1,128)} %s_ref.1), custom_call_target="tpu_custom_call" | custom-call | tf_op jit(solution)/shard_map/schur/pallas_call | solution.py:567
